TPU v7x, 32 devices: a whole 2x2x4 slice. The times are simulated.
32 devices in a mesh: dp: 8 (over y, x, core), tensor: 4 (over z).
Axes of the slice: x: 2, y: 2, z: 4, core: 2. Of those that a mesh axis runs over, the one named last changes fastest.
Arguments:
- tokens_in: bfloat16 [12288, 768], P('dp'), may hold values from -6 to 6
- segment_ids: int32 [8, 1536], P('dp'), may hold values from 0 to 11, never falling along the last dimension, each value on 1 to 216 neighbouring positions
- first_gain: float32 [768], replicated, may hold values from 0.25 to 1.75
- first_shift: float32 [768], replicated, may hold values from -3 to 3
- qkv_weight: bfloat16 [3, 768, 768], P(None, None, 'tensor'), may hold values from -0.21875 to 0.21875
- query_value_bias: float32 [2, 768], P(None, 'tensor'), may hold values from -1.2 to 1.2
- out_weight: bfloat16 [768, 768], P('tensor'), may hold values from -0.875 to 0.875
- out_bias: float32 [768], replicated, may hold values from -3 to 3
- second_gain: float32 [768], replicated, may hold values from 0.25 to 1.75
- second_shift: float32 [768], replicated, may hold values from -3 to 3
- up_weight: bfloat16 [768, 3072], P(None, 'tensor'), may hold values from -0.21875 to 0.21875
- up_bias: float32 [3072], P('tensor'), may hold values from -3 to 3
- down_weight: bfloat16 [3072, 768], P('tensor'), may hold values from -0.109375 to 0.109375
- down_bias: float32 [768], replicated, may hold values from -3 to 3
- cotangent: bfloat16 [12288, 768], P('dp'), may hold values from -6 to 6
Outputs:
- result: bfloat16 [12288, 768], P('dp')
- input_grad: bfloat16 [12288, 768], P('dp')
- first_gain_grad: float32 [768], replicated
- first_shift_grad: float32 [768], replicated
- qkv_weight_grad: float32 [3, 768, 768], P(None, None, 'tensor')
- query_value_bias_grad: float32 [2, 768], P(None, 'tensor')
- out_weight_grad: float32 [768, 768], P('tensor')
- out_bias_grad: float32 [768], replicated
- second_gain_grad: float32 [768], replicated
- second_shift_grad: float32 [768], replicated
- up_weight_grad: float32 [768, 3072], P(None, 'tensor')
- up_bias_grad: float32 [3072], P('tensor')
- down_weight_grad: float32 [3072, 768], P('tensor')
- down_bias_grad: float32 [768], replicated
Inputs may be any that keep to these rules, and one draw needn't show every extreme that they name: `segment_ids`: in each sequence the ids never fall; each crop holds 1 to 216 tokens, one exactly 216.
All inputs are finite; a program needn't handle non-finite values.
Results may differ from a plain program's by a relative error of at most 0.018.
Values may be sent and summed in bfloat16 or wider, within the bound.
A program may use at most 192 MiB of HBM per device.

v0:
```python
import jax
import jax.numpy as jnp
from jax import lax
from jax.sharding import PartitionSpec as P

HEAD_DIM = 64


norm_eps = 1e-06


def layer_norm(inputs, scaling, offset):
    center = inputs - jnp.mean(inputs, axis=-1, keepdims=True)
    spread = jnp.mean(center * center, axis=-1, keepdims=True)
    return center * lax.rsqrt(spread + norm_eps) * scaling + offset


def gelu_exact(inputs):
    return jax.nn.gelu(inputs, approximate=False)


def score_block(query_rows, segment_rows, key_all, segment_all):
    scores = jnp.einsum(
        "qhd,khd->hqk", query_rows, key_all, preferred_element_type=jnp.float32
    ) * HEAD_DIM ** (-0.5)
    allowed = segment_rows[:, None] == segment_all[None, :]
    return jnp.where(allowed[None], scores, -1000000000.0)


def body(
    tokens_in,
    segment_ids,
    first_gain,
    first_shift,
    qkv_weight,
    query_value_bias,
    out_weight,
    out_bias,
    second_gain,
    second_shift,
    up_weight,
    up_bias,
    down_weight,
    down_bias,
    cotangent,
):
    tokens = tokens_in.astype(jnp.float32)
    segments = segment_ids[0]
    length = tokens.shape[0]
    local_width = qkv_weight.shape[2]
    local_heads = local_width // HEAD_DIM
    block_rows = min(512, length)
    count_blocks = length // block_rows
    scale_factor = HEAD_DIM ** (-0.5)
    normed_full, first_back = jax.vjp(layer_norm, tokens, first_gain, first_shift)
    normed = normed_full.astype(jnp.bfloat16)
    projected = jnp.einsum("td,sdc->stc", normed, qkv_weight, preferred_element_type=jnp.float32)
    heads_shape = (length, local_heads, HEAD_DIM)
    query_all = (projected[0] + query_value_bias[0]).astype(jnp.bfloat16).reshape(heads_shape)
    key_all = projected[1].astype(jnp.bfloat16).reshape(heads_shape)
    value_all = (projected[2] + query_value_bias[1]).astype(jnp.bfloat16).reshape(heads_shape)
    query_blocks = query_all.reshape(count_blocks, block_rows, local_heads, HEAD_DIM)
    segment_blocks = segments.reshape(count_blocks, block_rows)

    def forward_block(operands):
        query_rows, segment_rows = operands
        scores = score_block(query_rows, segment_rows, key_all, segments)
        row_max = jnp.max(scores, axis=-1, keepdims=True)
        shifted = jnp.exp(scores - row_max)
        row_total = jnp.sum(shifted, axis=-1, keepdims=True)
        probs_low = (shifted / row_total).astype(jnp.bfloat16)
        mixed_rows = jnp.einsum(
            "hqk,khd->qhd", probs_low, value_all, preferred_element_type=jnp.float32
        )
        return (mixed_rows, row_max + jnp.log(row_total))

    mixed_rows, log_sums = lax.map(forward_block, (query_blocks, segment_blocks))
    heads_out = mixed_rows.reshape(length, local_width).astype(jnp.bfloat16)
    branch = lax.psum(
        jnp.dot(heads_out, out_weight, preferred_element_type=jnp.float32).astype(jnp.bfloat16),
        "tensor",
    ).astype(jnp.float32)
    hidden = tokens + branch + out_bias
    normed_two_full, second_back = jax.vjp(layer_norm, hidden, second_gain, second_shift)
    normed_two = normed_two_full.astype(jnp.bfloat16)
    pre_act = jnp.dot(normed_two, up_weight, preferred_element_type=jnp.float32) + up_bias
    activated_full, gelu_back = jax.vjp(gelu_exact, pre_act)
    activated = activated_full.astype(jnp.bfloat16)
    mlp_out = lax.psum(
        jnp.dot(activated, down_weight, preferred_element_type=jnp.float32).astype(jnp.bfloat16),
        "tensor",
    ).astype(jnp.float32)
    result = (hidden + mlp_out + down_bias).astype(jnp.bfloat16)
    grad_out = cotangent.astype(jnp.float32)
    down_weight_grad = jnp.einsum(
        "tf,td->fd", activated, cotangent, preferred_element_type=jnp.float32
    )
    down_bias_grad = jnp.sum(grad_out, axis=0)
    grad_act = jnp.einsum("td,fd->tf", cotangent, down_weight, preferred_element_type=jnp.float32)
    grad_pre = gelu_back(grad_act)[0].astype(jnp.bfloat16)
    up_bias_grad = jnp.sum(grad_pre.astype(jnp.float32), axis=0)
    up_weight_grad = jnp.einsum(
        "td,tf->df", normed_two, grad_pre, preferred_element_type=jnp.float32
    )
    grad_normed_two = lax.psum(
        jnp.einsum("tf,df->td", grad_pre, up_weight, preferred_element_type=jnp.float32).astype(
            jnp.bfloat16
        ),
        "tensor",
    ).astype(jnp.float32)
    grad_hidden_norm, second_gain_grad, second_shift_grad = second_back(grad_normed_two)
    grad_hidden = grad_out + grad_hidden_norm
    out_bias_grad = jnp.sum(grad_hidden, axis=0)
    grad_branch = grad_hidden.astype(jnp.bfloat16)
    out_weight_grad = jnp.einsum(
        "tc,td->cd", heads_out, grad_branch, preferred_element_type=jnp.float32
    )
    grad_heads = jnp.einsum(
        "td,cd->tc", grad_branch, out_weight, preferred_element_type=jnp.float32
    ).astype(jnp.bfloat16)
    grad_blocks = grad_heads.reshape(count_blocks, block_rows, local_heads, HEAD_DIM)

    def backward_block(carried, operands):
        grad_keys, grad_values = carried
        query_rows, segment_rows, grad_rows, log_rows = operands
        scores = score_block(query_rows, segment_rows, key_all, segments)
        probs_full = jnp.exp(scores - log_rows)
        probs_low = probs_full.astype(jnp.bfloat16)
        grad_values = grad_values + jnp.einsum(
            "hqk,qhd->khd", probs_low, grad_rows, preferred_element_type=jnp.float32
        )
        grad_probs = jnp.einsum(
            "qhd,khd->hqk", grad_rows, value_all, preferred_element_type=jnp.float32
        )
        row_inner = jnp.sum(probs_full * grad_probs, axis=-1, keepdims=True)
        grad_scores = (probs_full * (grad_probs - row_inner)).astype(jnp.bfloat16)
        grad_query = (
            jnp.einsum("hqk,khd->qhd", grad_scores, key_all, preferred_element_type=jnp.float32)
            * scale_factor
        )
        grad_keys = (
            grad_keys
            + jnp.einsum(
                "hqk,qhd->khd", grad_scores, query_rows, preferred_element_type=jnp.float32
            )
            * scale_factor
        )
        return ((grad_keys, grad_values), grad_query)

    zero_grads = jnp.zeros(heads_shape, jnp.float32)
    (grad_keys, grad_values), grad_queries = lax.scan(
        backward_block,
        (zero_grads, zero_grads),
        (query_blocks, segment_blocks, grad_blocks, log_sums),
    )
    grad_qkv = jnp.stack(
        [
            grad_queries.reshape(length, local_width),
            grad_keys.reshape(length, local_width),
            grad_values.reshape(length, local_width),
        ]
    ).astype(jnp.bfloat16)
    qkv_weight_grad = jnp.einsum(
        "td,stc->sdc", normed, grad_qkv, preferred_element_type=jnp.float32
    )
    query_value_bias_grad = jnp.stack(
        [
            jnp.sum(grad_qkv[0].astype(jnp.float32), axis=0),
            jnp.sum(grad_qkv[2].astype(jnp.float32), axis=0),
        ]
    )
    grad_normed = lax.psum(
        jnp.einsum("stc,sdc->td", grad_qkv, qkv_weight, preferred_element_type=jnp.float32).astype(
            jnp.bfloat16
        ),
        "tensor",
    ).astype(jnp.float32)
    grad_tokens_norm, first_gain_grad, first_shift_grad = first_back(grad_normed)
    input_grad = (grad_hidden + grad_tokens_norm).astype(jnp.bfloat16)
    (
        first_gain_grad,
        first_shift_grad,
        qkv_weight_grad,
        query_value_bias_grad,
        out_weight_grad,
        out_bias_grad,
        down_weight_grad,
        down_bias_grad,
        up_weight_grad,
        up_bias_grad,
        second_gain_grad,
        second_shift_grad,
    ) = lax.psum(
        (
            first_gain_grad,
            first_shift_grad,
            qkv_weight_grad,
            query_value_bias_grad,
            out_weight_grad,
            out_bias_grad,
            down_weight_grad,
            down_bias_grad,
            up_weight_grad,
            up_bias_grad,
            second_gain_grad,
            second_shift_grad,
        ),
        "dp",
    )
    replicas = float(lax.axis_size("dp"))
    return (
        result,
        input_grad,
        first_gain_grad / replicas,
        first_shift_grad / replicas,
        qkv_weight_grad / replicas,
        query_value_bias_grad / replicas,
        out_weight_grad / replicas,
        out_bias_grad / replicas,
        second_gain_grad / replicas,
        second_shift_grad / replicas,
        up_weight_grad / replicas,
        up_bias_grad / replicas,
        down_weight_grad / replicas,
        down_bias_grad / replicas,
    )


def solution(mesh):
    placed = (
        P("dp", None),
        P("dp", None),
        P(),
        P(),
        P(None, None, "tensor"),
        P(None, "tensor"),
        P("tensor", None),
        P(),
        P(),
        P(),
        P(None, "tensor"),
        P("tensor"),
        P("tensor", None),
        P(),
        P("dp", None),
    )
    return jax.shard_map(
        body,
        mesh=mesh,
        in_specs=placed,
        out_specs=(
            P("dp", None),
            P("dp", None),
            P(),
            P(),
            P(None, None, "tensor"),
            P(None, "tensor"),
            P("tensor", None),
            P(),
            P(),
            P(),
            P(None, "tensor"),
            P("tensor"),
            P("tensor", None),
            P(),
        ),
        check_vma=False,
    )
```

profile of v0, /device:TPU:0, one launch (start us, length us, event | category | flops | bytes accessed | tf_op | source)
XLA Modules:
  0.0 774.6 jit_solution(7280475762068593791)
XLA Ops:
  19.7 2.8 squeeze.24
  28.3 38.8 %while.27 = (s32[]{:T(128)}, bf16[3,512,3,64]{1,3,2,0:T(8,128)(2,1)}, f32[3,3,512,1]{2,1,3,0:T(4,128)}, s32[3,512]{1,0:T(4,128)}, s32[1,1536]{1,0:T(1,128)S(1)},...) while((s32[]{:T(128)}, ...), condition=%wide.region_5.6_spmd, body=%wide.region_2.5_spmd.sunk | while | flops 633076224 | bytes 40384724 | solution.py:77
  30.8 3.2 fusion.128
  34.0 2.8 fusion.129
  36.8 3.6 fusion.130
  43.7 3.2 fusion.128
  46.9 2.8 fusion.129
  49.7 3.6 fusion.130
  56.7 3.2 fusion.128
  59.9 2.8 fusion.129
  62.7 3.6 fusion.130
  69.7 3.2 convolution_convert_fusion.2
  72.9 9.8 %all-reduce.10.cloned.1.call-start = ((), (), s32[]{:S(2)}) async-start(), calls=%async_computation.1 | async-start | bytes 4718592 | tf_op jit(solution)/shard_map/psum | solution.py:105
  82.7 88.7 %all-reduce.8.cloned.1.call-done = bf16[1536,768]{1,0:T(8,128)(2,1)} async-done(((bf16[1536,768]{1,0:T(8,128)(2,1)}), bf16[1536,768]{1,0:T(8,128)(2,1)}) %all-reduce.8.cloned.1.call-update) | async-done | bytes 2359312 | tf_op jit(solution)/shard_map/psum | solution.py:79
  171.4 2.6 fusion.59
  176.7 3.7 fusion.75
  180.5 14.7 %convert_reduce_fusion.4 = (f32[768]{0:T(1024)}, bf16[1536,768]{1,0:T(8,128)(2,1)S(1)}, f32[1536,768]{1,0:T(8,128)}) fusion(f32[1536,768]{1,0:T(8,128)S(1)} %fusion.75, f32[768]{0:T(1024)S(1)} %copy-done.59, bf16[1536,768]{1,0:T(8,128)(2,1)S(1)} %copy-done.15, bf16[768,768]{1,0:T(8,128)(2,1)S(1)} %copy-done), kind=kOutput, calls=%fused_computation.78 | convolution fusion | flops 1900412160 | bytes 15341568 | tf_op jit(solution)/shard_map/td,fd->tf/dot_general | solution.py:99
  196.5 3.5 convolution_convert_fusion
  200.1 4.6 multiply_convert_fusion.1
  204.8 3.5 fusion.84
  208.4 4.3 fusion.74
  212.7 82.1 %all-reduce.10.cloned.1.call-done = bf16[1536,768]{1,0:T(8,128)(2,1)} async-done(((bf16[1536,768]{1,0:T(8,128)(2,1)}), bf16[1536,768]{1,0:T(8,128)(2,1)}) %all-reduce.10.cloned.1.call-update) | async-done | bytes 2359312 | tf_op jit(solution)/shard_map/psum | solution.py:105
  294.9 5.5 convert_reduce_fusion.1
  300.5 4.1 fusion.51
  304.5 3.6 fusion.82
  317.3 102.2 %while.28 = (s32[]{:T(128)}, f32[1536,3,64]{0,2,1:T(8,128)}, f32[1536,3,64]{0,2,1:T(8,128)}, bf16[3,512,3,64]{1,3,2,0:T(8,128)(2,1)}, bf16[3,512,3,64]{1,3,2,0:T...) while((s32[]{:T(128)}, f32[1536,3,64]{0,2,1:T(8,128)}, ...), condition=%wide.region_15.16_spmd.clone, body=%wide.region_13.15_spmd.clone.sunk | while | flops 1533540864 | bytes 155621840 | solution.py:151
  321.2 2.6 fusion.140
  323.9 7.2 multiply_reduce_fusion.3
  331.1 9.5 %multiply_convert_fusion.3 = bf16[3,512,1536]{2,1,0:T(8,128)(2,1)} fusion(f32[3,512,1536]{2,1,0:T(8,128)} %get-tuple-element.393, f32[3,512,1536]{2,1,0:T(8,128)} %copy-done.1, f32[3,512]{1,0:T(4,128)S(1)} %get-tuple-element.394), kind=kLoop, calls=%fused_computation.17.clone.1 | loop fusion | flops 7077888 | bytes 23599104 | tf_op jit(solution)/shard_map/while/body/eval_jaxpr/convert_element_type | solution.py:136
  340.5 5.9 fusion.142
  355.1 2.6 fusion.140
  357.8 7.2 multiply_reduce_fusion.3
  365.0 9.5 %multiply_convert_fusion.3 = bf16[3,512,1536]{2,1,0:T(8,128)(2,1)} fusion(f32[3,512,1536]{2,1,0:T(8,128)} %get-tuple-element.393, f32[3,512,1536]{2,1,0:T(8,128)} %copy-done.1, f32[3,512]{1,0:T(4,128)S(1)} %get-tuple-element.394), kind=kLoop, calls=%fused_computation.17.clone.1 | loop fusion | flops 7077888 | bytes 23599104 | tf_op jit(solution)/shard_map/while/body/eval_jaxpr/convert_element_type | solution.py:136
  374.4 6.1 fusion.142
  391.9 7.2 multiply_reduce_fusion.3
  399.1 9.5 %multiply_convert_fusion.3 = bf16[3,512,1536]{2,1,0:T(8,128)(2,1)} fusion(f32[3,512,1536]{2,1,0:T(8,128)} %get-tuple-element.393, f32[3,512,1536]{2,1,0:T(8,128)} %copy-done.1, f32[3,512]{1,0:T(4,128)S(1)} %get-tuple-element.394), kind=kLoop, calls=%fused_computation.17.clone.1 | loop fusion | flops 7077888 | bytes 23599104 | tf_op jit(solution)/shard_map/while/body/eval_jaxpr/convert_element_type | solution.py:136
  408.6 6.1 fusion.142
  422.0 2.7 stack_reshape.12
  428.4 4.1 fusion.63
  432.6 5.4 convolution_convert_fusion.1
  438.1 3.5 bitcast_convert_fusion
  444.6 100.5 %all-reduce.12.cloned.1.call-done = (f32[3,768,192]{1,2,0:T(8,128)}, f32[192,768]{1,0:T(8,128)}, f32[768,768]{1,0:T(8,128)}, f32[768,768]{1,0:T(8,128)}) async-done(((f32[3,768,192]{1,2,0:T(8,128)}, f32[192,768]{1,0:T(8,128)}, f32[768,768]{1,0:T(8,128)}, f32[768,768]{1,0:T(8,128)}), (f32[3,768,192]{1,2,0:T(8,128)}, f32[192,768]{1,0:T(8,128)}, f32[768,768]{1,0:T(8,128)}, ...) | async-done | bytes 7077904 | tf_op jit(solution)/shard_map/psum | solution.py:193
  547.3 2.8 broadcast_multiply_fusion.2
  552.6 167.9 %all-reduce.14.cloned.1.call-done = (bf16[1536,768]{1,0:T(8,128)(2,1)}, bf16[1536,768]{1,0:T(8,128)(2,1)}) async-done(((bf16[1536,768]{1,0:T(8,128)(2,1)}, bf16[1536,768]{1,0:T(8,128)(2,1)}), (bf16[1536,768]{1,0:T(8,128)(2,1)}, bf16[1536,768]{1,0:T(8,128)(2,1)})) %all-reduce.14.cloned.1.call-update) | async-done | bytes 4718608 | tf_op jit(solution)/shard_map/psum | solution.py:89
  720.5 4.1 convert_reduce_fusion
  724.7 3.4 fusion.52
  728.1 25.3 %all-reduce = (f32[768]{0:T(1024)}, f32[768]{0:T(1024)}, f32[2,192]{1,0:T(2,128)}, f32[768]{0:T(1024)}, f32[768]{0:T(1024)}, /*index=5*/f32[768]{0:T(1024)}, f32[768]{0:T(1024)}, f32[768]{0:T(1024)}) all-reduce(f32[768]{0:T(1024)} %get-tuple-element.189, f32[768]{0:T(1024)} %get-tuple-element.193, ...), channel_id=1, replica_groups=mesh['dp'=8,'tensor'=4] {'dp'}, use_global_device_ids=true, to_apply=%region_20.21 | all-reduce | flops 5760 | bytes 46080 | tf_op jit(solution)/shard_map/psum | solution.py:193
  760.5 7.3 add_convert_fusion
  (270 shorter events, 93.6 us)
Async XLA Ops:
  7.2 173.2 %copy-start = (bf16[768,768]{1,0:T(8,128)(2,1)S(1)}, bf16[768,768]{1,0:T(8,128)(2,1)}, u32[]{:S(2)}) copy-start(bf16[768,768]{1,0:T(8,128)(2,1)} %param.31) | copy-start | bytes 3538948
  7.2 5.4 copy-start.3
  7.2 5.4 copy-start.54
  7.2 5.4 copy-start.64
  7.2 164.2 %all-reduce.8.cloned.1.call-start = ((), (), s32[]{:S(2)}) async-start(), calls=%async_computation | async-start | bytes 4718592 | tf_op jit(solution)/shard_map/psum | solution.py:79
  7.3 5.3 copy-start.61
  9.5 5.0 copy-start.37
  14.5 4.5 copy-start.32
  19.7 5.6 copy-start.58
  67.1 104.3 %copy-start.39 = (f32[768]{0:T(1024)S(1)}, f32[768]{0:T(1024)}, u32[]{:S(2)}) copy-start(f32[768]{0:T(1024)} %param.26) | copy-start | bytes 9220
  72.9 221.9 %all-reduce.10.cloned.1.call-start = ((), (), s32[]{:S(2)}) async-start(), calls=%async_computation.1 | async-start | bytes 4718592 | tf_op jit(solution)/shard_map/psum | solution.py:105
  171.4 5.2 copy-start.60
  180.5 14.7 %copy-start.21 = (f32[1536,768]{1,0:T(8,128)}, f32[1536,768]{1,0:T(8,128)S(1)}, u32[]{:S(2)}) copy-start(f32[1536,768]{1,0:T(8,128)S(1)} %fusion.75) | copy-start | bytes 14155780
  200.0 345.2 %all-reduce.12.cloned.1.call-start = ((), (), s32[]{:S(2)}) async-start(), calls=%async_computation.2 | async-start | bytes 14155776 | tf_op jit(solution)/shard_map/psum | solution.py:193
  200.1 4.6 copy-start.16
  294.8 5.6 copy-start.50
  294.8 5.6 copy-start.8
  294.8 5.6 copy-start.14
  294.8 5.6 copy-start.41
  294.8 5.6 copy-start.53
  294.8 5.6 copy-start.57
  300.4 4.1 copy-start.17
  323.9 7.2 copy-start.1
  340.5 5.9 copy-start.2
  340.5 5.9 copy-start.5
  340.5 5.9 copy-start.25
  357.8 7.2 copy-start.1
  374.4 6.2 copy-start.2
  374.4 6.2 copy-start.5
  374.4 6.2 copy-start.25
  391.9 7.2 copy-start.1
  408.6 6.2 copy-start.2
  408.6 6.2 copy-start.5
  408.6 6.2 copy-start.25
  419.5 8.9 %copy-start.38 = (f32[1536]{0:T(1024)S(1)}, f32[1536]{0:T(1024)}, u32[]{:S(2)}) copy-start(f32[1536]{0:T(1024)} %copy-done.37) | copy-start | bytes 18436
  419.5 8.9 %copy-start.45 = (f32[1536]{0:T(1024)S(1)}, f32[1536]{0:T(1024)}, u32[]{:S(2)}) copy-start(f32[1536]{0:T(1024)} %copy-done.44) | copy-start | bytes 18436
  432.5 288.0 %all-reduce.14.cloned.1.call-start = ((), (), s32[]{:S(2)}) async-start(), calls=%async_computation.3 | async-start | bytes 9437184 | tf_op jit(solution)/shard_map/psum | solution.py:89
  432.6 5.5 copy-start.23
  432.6 5.4 copy-start.24
  432.6 5.4 copy-start.36
  432.6 5.4 copy-start.62
  545.2 4.9 copy-start.29
  545.2 4.9 copy-start.30
  550.1 170.4 %copy-start.55 = (f32[768]{0:T(1024)S(1)}, f32[768]{0:T(1024)}, u32[]{:S(2)}) copy-start(f32[768]{0:T(1024)} %param.21) | copy-start | bytes 9220
  720.5 4.1 copy-start.48
  720.5 4.1 copy-start.13
  720.5 4.1 copy-start.46
  720.5 40.0 %copy-start.42 = (f32[768]{0:T(1024)S(1)}, f32[768]{0:T(1024)}, u32[]{:S(2)}) copy-start(f32[768]{0:T(1024)} %param.26) | copy-start | bytes 9220
  (49 other events, 113.5 us)
Sparse Core Ops, SparseCore 0:
  73.0 98.3 all-reduce.7
  200.1 94.6 all-reduce.9
  432.7 112.4 all-reduce.11
  548.0 172.4 all-reduce.13
where the time goes:
time: 784 us; the launch traced here: 775 us
  waiting for transfers between devices  439 us (56%)
  matrix products  130 us (17%)
  other arithmetic  115 us (15%)
  local copies, waits for them, and re-layouts  40 us (5%)
  blocking collectives  25.3 us (3%)
  between operations  14.5 us (2%)
  starting transfers between devices  9.94 us (1%)
    psum x1, waiting for transfers between devices, body(): lax.psum(jnp.dot(activated, down_weight, preferred_element_type=jnp.float...  168 us
    psum x1, waiting for transfers between devices, body(): lax.psum((first_gain_grad, first_shift_grad, qkv_weight_grad, query_value...  101 us
    psum x1, waiting for transfers between devices, body(): lax.psum(jnp.dot(heads_out, out_weight, preferred_element_type=jnp.float3...  88.7 us
    psum x1, waiting for transfers between devices, body(): lax.psum(jnp.einsum('tf,df->td', grad_pre, up_weight, preferred_element_t...  82.1 us
    dot_general x6, matrix products, score_block(): jnp.einsum('qhd,khd->hqk', query_rows, key_all, preferred_element_type=jn...  31.1 us
    convert_element_type x3, other arithmetic, backward_block(): grad_scores = (probs_full * (grad_probs - row_inner)).astype(jnp.bfloat16)  28.4 us
    psum x1, blocking collectives, body(): lax.psum((first_gain_grad, first_shift_grad, qkv_weight_grad, query_value...  25.3 us
    dot_general x3, matrix products, backward_block(): jnp.einsum('hqk,qhd->khd', probs_low, grad_rows, preferred_element_type=j...  18.2 us
  transfers between devices with their start and end apart: 4, of which 4 were waited for; matrix products, arithmetic and copies ran while one was open for 4% of the time, Pallas kernels for 0%

commit v1 on v0

v1 whole, which is shorter than its diff:
```python
import functools

import jax
import jax.numpy as jnp
from jax import lax
from jax.experimental import pallas as pl
from jax.experimental.pallas import tpu as pltpu
from jax.sharding import PartitionSpec as P

HEAD_DIM = 64
HALO = 256
BLOCK = 128
EPS = 1e-06
F32 = jnp.float32
BF16 = jnp.bfloat16
MESH = pl.DeviceIdType.MESH
VMEM_LIMIT = 60 << 20


def place():
    d, t = lax.axis_index("dp"), lax.axis_index("tensor")
    return d, t, lax.rem(d, 2), lax.rem(d // 2, 2), lax.rem(d // 4, 2)


def flip(d, value):
    return d + value * (1 - 2 * lax.rem(d // value, 2))


def remote(src, dst, send, recv, **axis):
    return pltpu.make_async_remote_copy(
        src_ref=src, dst_ref=dst, send_sem=send, recv_sem=recv,
        device_id=axis, device_id_type=MESH)


def greet(nt, bits, far=False):
    d, t = lax.axis_index("dp"), lax.axis_index("tensor")
    barrier = pltpu.get_barrier_semaphore()

    @pl.when(t > 0)
    def _():
        pl.semaphore_signal(barrier, inc=1, device_id={"tensor": t - 1}, device_id_type=MESH)

    @pl.when(t < nt - 1)
    def _():
        pl.semaphore_signal(barrier, inc=1, device_id={"tensor": t + 1}, device_id_type=MESH)

    for bit in bits:
        pl.semaphore_signal(barrier, inc=1, device_id={"dp": flip(d, bit)}, device_id_type=MESH)
    if far:
        pl.semaphore_signal(barrier, inc=1, device_id={"tensor": flip(t, 2)}, device_id_type=MESH)
    peers = len(bits) + int(far) + (t > 0).astype(jnp.int32) + (t < nt - 1).astype(jnp.int32)
    pl.semaphore_wait(barrier, peers)


def ordered(tasks):
    for _, _, task in sorted(tasks, key=lambda item: item[:2]):
        task()


def relay_tasks(nt, chunks, own, full, sems, start, hop, place_of, arrived):
    send, recv = sems
    tasks = []
    t = lax.axis_index("tensor")
    for k in range(chunks):
        for j in range(nt):
            def step(k=k, j=j):
                for way in (0, 1):
                    sign = 1 - 2 * way
                    shard = t - sign * j
                    inside = (shard >= 0) & (shard < nt)
                    if j > 0:
                        @pl.when(inside)
                        def _():
                            remote(full(shard, k), full(shard, k), send.at[k, j - 1, way], recv.at[k, j - 1, way],
                                   tensor=t).wait_recv()
                            arrived(k, j, way, shard)
                    if j < nt - 1:
                        goal = t + sign
                        @pl.when(inside & (goal >= 0) & (goal < nt))
                        def _():
                            source = own(k) if j == 0 else full(shard, k)
                            remote(source, full(shard, k), send.at[k, j, way], recv.at[k, j, way],
                                   tensor=goal).start()
            tasks.append((start(k, j), len(tasks), step))

    def finish():
        for k in range(chunks):
            for j in range(nt - 1):
                for way in (0, 1):
                    sign = 1 - 2 * way
                    shard, goal = t - sign * j, t + sign
                    @pl.when((shard >= 0) & (shard < nt) & (goal >= 0) & (goal < nt))
                    def _():
                        source = own(k) if j == 0 else full(shard, k)
                        remote(source, full(shard, k), send.at[k, j, way], recv.at[k, j, way],
                               tensor=goal).wait_send()
    return tasks, finish


def gather_kernel(nt, chunks, pack, w, zs, zr, ps, pr, cs, cr, ls):
    d, t, b0, b1, b2 = place()
    local = pltpu.make_async_copy(pack, w.at[t], ls)
    local.start()
    greet(nt, (1, 2, 4))
    tasks = []

    def one(shard, k, q, way, j):
        if q == 0:
            return remote(w.at[shard, k, b0, b2, b1, 0], w.at[shard, k, b0, b2, b1, 0],
                       ps.at[k, j, way, 0], pr.at[k, j, way, 0], dp=flip(d, 2))
        return remote(w.at[shard, k, b0, b2, b1, 1], w.at[shard, k, b0, b2, b1, 1],
                   ps.at[k, j, way, 1], pr.at[k, j, way, 1], dp=flip(d, 4))

    def two(shard, k, q, way, j):
        if q == 0:
            return remote(w.at[shard, k, b0, b2, :, 0], w.at[shard, k, b0, b2, :, 0],
                       ps.at[k, j, way, 2], pr.at[k, j, way, 2], dp=flip(d, 4))
        return remote(w.at[shard, k, b0, :, b1, 1], w.at[shard, k, b0, :, b1, 1],
                   ps.at[k, j, way, 3], pr.at[k, j, way, 3], dp=flip(d, 2))

    def core(shard, k, way, j):
        return remote(w.at[shard, k, b0], w.at[shard, k, b0], cs.at[k, j, way], cr.at[k, j, way], dp=flip(d, 1))

    def arrived(k, j, way, shard):
        one(shard, k, 0, way, j - 1).start()
        one(shard, k, 1, way, j - 1).start()

    def each(k, j, body):
        for way in (0, 1):
            shard = t - (1 - 2 * way) * (j + 1)
            @pl.when((shard >= 0) & (shard < nt))
            def _():
                body(shard, k, way, j)

    z_tasks, z_finish = relay_tasks(
        nt, chunks, lambda k: pack.at[k, b0, b2, b1], lambda s, k: w.at[s, k, b0, b2, b1], (zs, zr),
        lambda k, j: 16.0 * k + 4.0 * j, None, None, arrived)
    tasks += z_tasks
    for k in range(chunks):
        for j in range(nt - 1):
            def second(k=k, j=j):
                def body(shard, k, way, j):
                    for q in (0, 1):
                        one(shard, k, q, way, j).wait_recv()
                    for q in (0, 1):
                        two(shard, k, q, way, j).start()
                each(k, j, body)

            def third(k=k, j=j):
                def body(shard, k, way, j):
                    for q in (0, 1):
                        two(shard, k, q, way, j).wait_recv()
                    core(shard, k, way, j).start()
                each(k, j, body)
            tasks.append((16.0 * k + 4.0 * j + 9.0, len(tasks), second))
            tasks.append((16.0 * k + 4.0 * j + 16.5, len(tasks), third))
    ordered(tasks)
    local.wait()
    z_finish()
    for k in range(chunks):
        for j in range(nt - 1):
            def last(shard, k, way, j):
                core(shard, k, way, j).wait()
                for q in (0, 1):
                    one(shard, k, q, way, j).wait_send()
                    two(shard, k, q, way, j).wait_send()
            each(k, j, last)


def gather_weights(pack, nt):
    chunks, rows = pack.shape[0], pack.shape[-2]
    width = pack.shape[-1]
    dma = pltpu.SemaphoreType.DMA
    return pl.pallas_call(
        functools.partial(gather_kernel, nt, chunks),
        name="gather_weights",
        out_shape=jax.ShapeDtypeStruct((nt,) + pack.shape, pack.dtype),
        in_specs=[pl.BlockSpec(memory_space=pl.ANY)],
        out_specs=pl.BlockSpec(memory_space=pltpu.VMEM),
        scratch_shapes=[
            dma((chunks, nt - 1, 2)), dma((chunks, nt - 1, 2)),
            dma((chunks, nt - 1, 2, 4)), dma((chunks, nt - 1, 2, 4)),
            dma((chunks, nt - 1, 2)), dma((chunks, nt - 1, 2)), dma(()),
        ],
        compiler_params=pltpu.CompilerParams(collective_id=1, has_side_effects=True, vmem_limit_bytes=VMEM_LIMIT),
    )(pack)


def add_bf16(ref, other):
    ref[...] = (ref[...].astype(F32) + other[...].astype(F32)).astype(BF16)


def reduce_kernel(nt, chunks, extra, outs, grads, small, own_rows, total, small_out, gathered,
                  s1, rc, ra, rb, rz, rx, sv, sr,
                  ls, cs, cr, ps, pr, zs, zr, xs, xr, fs, fr, os_, or_, ss, sm, lo):
    d, t, b0, b1, b2 = place()
    bits = (1, 2, 4) + tuple(extra)
    order = tuple(range(chunks))[::-1]
    units = [(k, s) for k in order for s in range(nt)]

    def own_copy(k, s):
        return pltpu.make_async_copy(grads.at[s, k, b0], s1.at[s, k], ls.at[s, k])

    for k, s in units:
        own_copy(k, s).start()
    own_small = pltpu.make_async_copy(small, sv, lo.at[0])
    own_small.start()
    keep = [pltpu.make_async_copy(own_rows.at[o], gathered.at[o, t], lo.at[1 + o]) for o in range(outs)]
    for copy in keep:
        copy.start()
    greet(nt, bits, nt > 2)

    def core(k, s):
        return remote(grads.at[s, k, 1 - b0], rc.at[s, k], cs.at[s, k], cr.at[s, k], dp=flip(d, 1))

    def one(k, s, q):
        if q == 0:
            return remote(s1.at[s, k, 1 - b2, :, 0], ra.at[s, k], ps.at[s, k, 0], pr.at[s, k, 0], dp=flip(d, 4))
        return remote(s1.at[s, k, :, 1 - b1, 1], rb.at[s, k], ps.at[s, k, 1], pr.at[s, k, 1], dp=flip(d, 2))

    def two(k, s, q):
        if q == 0:
            return remote(s1.at[s, k, b2, 1 - b1, 0], rz.at[s, k, 0], ps.at[s, k, 2], pr.at[s, k, 2], dp=flip(d, 2))
        return remote(s1.at[s, k, 1 - b2, b1, 1], rz.at[s, k, 1], ps.at[s, k, 3], pr.at[s, k, 3], dp=flip(d, 4))

    def up(k, s):
        return remote(s1.at[s, k, b2, b1], rx.at[s, k, 0], zs.at[s, k, 0], zr.at[s, k, 0], tensor=t + 1)

    def down(k, s):
        return remote(s1.at[s, k, b2, b1], rx.at[s, k, 1], zs.at[s, k, 1], zr.at[s, k, 1], tensor=t - 1)

    tasks = []

    def task(when, body):
        tasks.append((when, len(tasks), body))

    pace = 5.4
    for n, (k, s) in enumerate(units):
        def first(k=k, s=s):
            core(k, s).start()

        def second(k=k, s=s):
            own_copy(k, s).wait()
            core(k, s).wait_recv()
            add_bf16(s1.at[s, k], rc.at[s, k])
            one(k, s, 0).start()
            one(k, s, 1).start()

        def third(k=k, s=s):
            one(k, s, 0).wait_recv()
            one(k, s, 1).wait_recv()
            add_bf16(s1.at[s, k, b2, :, 0], ra.at[s, k])
            add_bf16(s1.at[s, k, :, b1, 1], rb.at[s, k])
            two(k, s, 0).start()
            two(k, s, 1).start()

        def fourth(k=k, s=s):
            two(k, s, 0).wait_recv()
            two(k, s, 1).wait_recv()
            add_bf16(s1.at[s, k, b2, b1, 0], rz.at[s, k, 0])
            add_bf16(s1.at[s, k, b2, b1, 1], rz.at[s, k, 1])
        task(n * pace - 12.0, first)
        task(n * pace, second)
        task(n * pace + 6.0, third)
        task(n * pace + 11.5, fourth)

    for c, k in enumerate(order):
        for hop in range(nt):
            def chain(k=k, hop=hop):
                @pl.when(t == hop)
                def _():
                    for s in reversed(range(nt)):
                        @pl.when(s >= t)
                        def _():
                            if hop > 0:
                                up(k, s).wait_recv()
                                add_bf16(s1.at[s, k, b2, b1], rx.at[s, k, 0])
                            if hop < nt - 1:
                                @pl.when(s > t)
                                def _():
                                    up(k, s).start()

                @pl.when(t == nt - 1 - hop)
                def _():
                    for s in range(nt):
                        @pl.when(s <= t)
                        def _():
                            if hop > 0:
                                down(k, s).wait_recv()
                                add_bf16(s1.at[s, k, b2, b1], rx.at[s, k, 1])
                            if hop < nt - 1:
                                @pl.when(s < t)
                                def _():
                                    down(k, s).start()
            task((c + 1) * nt * pace + 8.0 + 5.0 * hop, chain)

        def settle(k=k):
            pltpu.sync_copy(s1.at[t, k, b2, b1], total.at[k, b0, b2, b1])
        base = (c + 1) * nt * pace + 8.0 + 5.0 * nt
        if not extra:
            task(base, settle)
        else:
            for e, bit in enumerate(extra):
                def more(k=k, e=e, bit=bit):
                    swap = remote(s1.at[t, k, b2, b1], rx.at[e, k, 2], xs.at[e, k], xr.at[e, k], dp=flip(d, bit))
                    swap.start()
                    swap.wait()
                    add_bf16(s1.at[t, k, b2, b1], rx.at[e, k, 2])
                task(base + 0.01 * e, more)
            task(base + 0.5, settle)

        def gone(k, q):
            if q == 0:
                return remote(total.at[k, b0, b2, b1, 0], total.at[k, b0, b2, b1, 0], fs.at[k, 0], fr.at[k, 0], dp=flip(d, 2))
            return remote(total.at[k, b0, b2, b1, 1], total.at[k, b0, b2, b1, 1], fs.at[k, 1], fr.at[k, 1], dp=flip(d, 4))

        def gtwo(k, q):
            if q == 0:
                return remote(total.at[k, b0, b2, :, 0], total.at[k, b0, b2, :, 0], fs.at[k, 2], fr.at[k, 2], dp=flip(d, 4))
            return remote(total.at[k, b0, :, b1, 1], total.at[k, b0, :, b1, 1], fs.at[k, 3], fr.at[k, 3], dp=flip(d, 2))

        def gcore(k):
            return remote(total.at[k, b0], total.at[k, b0], fs.at[k, 4], fr.at[k, 4], dp=flip(d, 1))

        def spread_one(k=k):
            for q in (0, 1):
                gone(k, q).start()

        def spread_two(k=k):
            for q in (0, 1):
                gone(k, q).wait_recv()
            for q in (0, 1):
                gtwo(k, q).start()

        def spread_core(k=k):
            for q in (0, 1):
                gtwo(k, q).wait_recv()
            gcore(k).start()

        def spread_end(k=k):
            gcore(k).wait()
            for q in (0, 1):
                gone(k, q).wait_send()
                gtwo(k, q).wait_send()
        task(base + 1.0, spread_one)
        task(base + 4.0, spread_two)
        task(base + 8.0, spread_core)
        task(1e6, spread_end)

    z_tasks, z_finish = relay_tasks(
        nt, outs, lambda o: own_rows.at[o], lambda s, o: gathered.at[o, s], (os_, or_),
        lambda o, j: 1.0 + 46.0 * o + 14.0 * j, None, None, lambda *a: None)
    tasks += [(w, 1000 + n, b) for w, n, b in z_tasks]

    exchanges = [("dp", bit) for bit in bits]
    step = 1
    while step < nt:
        exchanges.append(("tensor", step))
        step *= 2
    for e, (axis, bit) in enumerate(exchanges):
        def swap(e=e, axis=axis, bit=bit):
            goal = {axis: flip(lax.axis_index(axis), bit)}
            return remote(sv, sr.at[e], ss.at[e], sm.at[e], **goal)

        def begin(e=e, swap=swap):
            if e == 0:
                own_small.wait()
            swap().start()

        def end(e=e, swap=swap):
            swap().wait()
            sv[...] = sv[...] + sr[e]
        task(2.0 + 6.0 * e, begin)
        task(6.0 + 6.0 * e, end)

    ordered(tasks)
    small_out[...] = sv[...]
    for copy in keep:
        copy.wait()
    z_finish()
    for k, s in units:
        core(k, s).wait_send()
        for q in (0, 1):
            one(k, s, q).wait_send()
            two(k, s, q).wait_send()

        @pl.when(s > t)
        def _():
            up(k, s).wait_send()

        @pl.when(s < t)
        def _():
            down(k, s).wait_send()


def reduce_grads(grads, small, own_rows, nt, extra):
    chunks, cols, outs = grads.shape[1], grads.shape[-1], own_rows.shape[0]
    dma = pltpu.SemaphoreType.DMA
    piece = grads.shape[-2]
    hops = 3 + len(extra) + (nt - 1).bit_length()
    any_ = pl.BlockSpec(memory_space=pl.ANY)
    return pl.pallas_call(
        functools.partial(reduce_kernel, nt, chunks, extra, outs),
        name="reduce_grads",
        out_shape=(
            jax.ShapeDtypeStruct(grads.shape[1:], BF16),
            jax.ShapeDtypeStruct(small.shape, F32),
            jax.ShapeDtypeStruct((outs, nt) + own_rows.shape[1:], BF16),
        ),
        in_specs=[any_, any_, any_],
        out_specs=(pl.BlockSpec(memory_space=pltpu.VMEM),) * 3,
        scratch_shapes=[
            pltpu.VMEM((nt, chunks, 2, 2, 2, piece, cols), BF16),
            pltpu.VMEM((nt, chunks, 2, 2, 2, piece, cols), BF16),
            pltpu.VMEM((nt, chunks, 2, piece, cols), BF16),
            pltpu.VMEM((nt, chunks, 2, piece, cols), BF16),
            pltpu.VMEM((nt, chunks, 2, piece, cols), BF16),
            pltpu.VMEM((nt, chunks, 3 if extra else 2, 2, piece, cols), BF16),
            pltpu.VMEM(small.shape, F32),
            pltpu.VMEM((hops,) + small.shape, F32),
            dma((nt, chunks)), dma((nt, chunks)), dma((nt, chunks)),
            dma((nt, chunks, 4)), dma((nt, chunks, 4)),
            dma((nt, chunks, 2)), dma((nt, chunks, 2)),
            dma((max(1, len(extra)), chunks)), dma((max(1, len(extra)), chunks)),
            dma((chunks, 5)), dma((chunks, 5)),
            dma((outs, nt - 1, 2)), dma((outs, nt - 1, 2)),
            dma((hops,)), dma((hops,)), dma((1 + outs,)),
        ],
        compiler_params=pltpu.CompilerParams(
            collective_id=2, has_side_effects=True, vmem_limit_bytes=VMEM_LIMIT),
    )(grads, small, own_rows)


def stacked(pair):
    lane = lax.broadcasted_iota(jnp.int32, pair.shape, 1)
    zero = jnp.zeros_like(pair)
    return jnp.concatenate([jnp.where(lane < HEAD_DIM, pair, zero), jnp.where(lane < HEAD_DIM, zero, pair)], axis=0)


def dot(a, b, dims):
    return lax.dot_general(a, b, (dims, ((), ())), preferred_element_type=F32)


NN = ((1,), (0,))
NT = ((1,), (1,))


def untangle(both):
    half = both.shape[1] // 2
    return jnp.concatenate([both[:HEAD_DIM, :half], both[HEAD_DIM:, half:]], axis=0).T


def attend_kernel(own, q_ref, k_ref, v_ref, segc, segr, o_ref, lse_ref):
    blocks = own // BLOCK
    for b in range(blocks):
        first, count = BLOCK * b, BLOCK + 2 * HALO
        q0 = HALO + BLOCK * b
        row = segr[:, q0:q0 + BLOCK]
        allowed = segc[first:first + count, :] == row
        allowed = jnp.concatenate([allowed, allowed], axis=1)

        def pair(j, carry):
            cols = pl.ds(pl.multiple_of(j * 128, 128), 128)
            q2 = stacked(q_ref[q0:q0 + BLOCK, cols])
            k2 = k_ref[first:first + count, cols]
            v2 = v_ref[first:first + count, cols]
            s = dot(k2, q2, NT) * (HEAD_DIM ** -0.5)
            s = jnp.where(allowed, s, -1e9)
            m = jnp.max(s, axis=0, keepdims=True)
            p = jnp.exp(s - m)
            l = jnp.sum(p, axis=0, keepdims=True)
            low = (p * (1.0 / l)).astype(BF16)
            out = dot(v2.T, low, NN)
            o_ref[b * BLOCK:(b + 1) * BLOCK, cols] = untangle(out).astype(BF16)
            lse_ref[j, b] = m + jnp.log(l)
            return carry
        lax.fori_loop(0, q_ref.shape[1] // 128, pair, 0)


def attend(q, k, v, segc, segr, own):
    width = q.shape[1]
    return pl.pallas_call(
        functools.partial(attend_kernel, own),
        name="attend",
        out_shape=(jax.ShapeDtypeStruct((own, width), BF16),
                   jax.ShapeDtypeStruct((width // 128, own // BLOCK, 1, 2 * BLOCK), F32)),
        compiler_params=pltpu.CompilerParams(vmem_limit_bytes=VMEM_LIMIT),
    )(q, k, v, segc, segr)


def attend_back_kernel(own, q_ref, k_ref, v_ref, g_ref, lse_ref, delta_ref, segc, segr, dq_ref, dk_ref, dv_ref, dk, dv):
    scale = HEAD_DIM ** -0.5
    window = own + 2 * HALO
    blocks = window // BLOCK
    mine = range(HALO // BLOCK, HALO // BLOCK + own // BLOCK)
    reach = HALO // BLOCK

    def pair(j, carry):
        cols = pl.ds(pl.multiple_of(j * 128, 128), 128)
        dk[...] = jnp.zeros_like(dk)
        dv[...] = jnp.zeros_like(dv)
        for w in range(blocks):
            low_block, high_block = max(0, w - reach), min(blocks, w + reach + 1)
            if w not in mine:
                low_block, high_block = max(low_block, mine[0]), min(high_block, mine[-1] + 1)
            k0, k1 = low_block * BLOCK, high_block * BLOCK
            q0 = w * BLOCK
            q2 = stacked(q_ref[q0:q0 + BLOCK, cols])
            g2 = stacked(g_ref[q0:q0 + BLOCK, cols])
            k2 = k_ref[k0:k1, cols]
            v2 = v_ref[k0:k1, cols]
            allowed = segc[k0:k1, :] == segr[:, q0:q0 + BLOCK]
            allowed = jnp.concatenate([allowed, allowed], axis=1)
            s = dot(k2, q2, NT) * scale
            p = jnp.exp(jnp.where(allowed, s - lse_ref[j, w], -1e9))
            low = p.astype(BF16)
            dp = dot(v2, g2, NT)
            ds = (p * (dp - delta_ref[j, w])).astype(BF16)
            o0, o1 = max(k0, HALO), min(k1, HALO + own)
            dst = slice(o0 - HALO, o1 - HALO)
            src = slice(o0 - k0, o1 - k0)
            dk[dst, :] += dot(ds[src], q2, NN)
            dv[dst, :] += dot(low[src], g2, NN)
            if w in mine:
                out = dot(k2.T, ds, NN)
                i = w - mine[0]
                dq_ref[i * BLOCK:(i + 1) * BLOCK, cols] = (untangle(out) * scale).astype(BF16)
        dk_ref[:, cols] = (dk[...] * scale).astype(BF16)
        dv_ref[:, cols] = dv[...].astype(BF16)
        return carry
    lax.fori_loop(0, q_ref.shape[1] // 128, pair, 0)


def attend_back(q, k, v, g, lse, delta, segc, segr, own):
    width = q.shape[1]
    shape = jax.ShapeDtypeStruct((own, width), BF16)
    return pl.pallas_call(
        functools.partial(attend_back_kernel, own),
        name="attend_back",
        out_shape=(shape, shape, shape),
        scratch_shapes=[pltpu.VMEM((own, 128), F32), pltpu.VMEM((own, 128), F32)],
        compiler_params=pltpu.CompilerParams(vmem_limit_bytes=VMEM_LIMIT),
    )(q, k, v, g, lse, delta, segc, segr)


def standardize(rows):
    center = rows - jnp.mean(rows, axis=-1, keepdims=True)
    r = lax.rsqrt(jnp.mean(center * center, axis=-1, keepdims=True) + EPS)
    return center * r, r


def norm_back(e, xhat, r):
    return r * (e - jnp.mean(e, axis=-1, keepdims=True) - xhat * jnp.mean(e * xhat, axis=-1, keepdims=True))


def body(tokens_in, segment_ids, first_gain, first_shift, qkv_weight, query_value_bias, out_weight, out_bias,
         second_gain, second_shift, up_weight, up_bias, down_weight, down_bias, cotangent):
    nt, ndp = lax.axis_size("tensor"), lax.axis_size("dp")
    t = lax.axis_index("tensor")
    length, width = tokens_in.shape
    own = length // nt
    local = qkv_weight.shape[2]
    hidden_local = up_weight.shape[1]
    start = t * own
    pack = jnp.concatenate([
        qkv_weight.transpose(0, 2, 1).reshape(3 * local, width), out_weight, up_weight, down_weight], axis=0)
    piece = width // 16
    pack = pack.reshape(-1, 2, 2, 2, 2, piece, width)
    chunks = pack.shape[0]
    whole = gather_weights(pack, nt).reshape(nt, chunks * width, width)
    up_all = lax.all_gather(up_bias, "tensor", tiled=True)
    qv_bias = lax.all_gather(query_value_bias, "tensor", axis=1, tiled=True)
    w_qkv = whole[:, :3 * local].reshape(nt, 3, local, width)
    w_out = whole[:, 3 * local:width]
    w_up = whole[:, width:2 * width]
    w_down = whole[:, 2 * width:]

    padded = jnp.pad(tokens_in, ((HALO, HALO), (0, 0)))
    tokens = lax.dynamic_slice_in_dim(padded, start, own + 2 * HALO).astype(F32)
    segs = lax.dynamic_slice_in_dim(jnp.pad(segment_ids[0], (HALO, HALO), constant_values=-1), start, own + 2 * HALO)
    segr = segs[None, :]
    segc = jnp.broadcast_to(segs[:, None], (own + 2 * HALO, BLOCK))
    cot = lax.dynamic_slice_in_dim(cotangent, start, own)
    xhat_all, r_all = standardize(tokens)
    normed = (xhat_all * first_gain + first_shift).astype(BF16)
    own_rows = slice(HALO, HALO + own)

    def project(s):
        return jnp.einsum("td,gcd->tgc", normed, w_qkv[:, s], preferred_element_type=F32).reshape(-1, width)
    q = (project(0) + qv_bias[0]).astype(BF16)
    k = project(1).astype(BF16)
    v = (project(2) + qv_bias[1]).astype(BF16)
    heads_out, lse = attend(q, k, v, segc, segr, own)
    heads_groups = heads_out.reshape(own, nt, local)
    branch = jnp.einsum("tgc,gcd->td", heads_groups, w_out, preferred_element_type=F32)
    hidden = tokens[own_rows] + branch + out_bias
    xhat2, r2 = standardize(hidden)
    normed_two = (xhat2 * second_gain + second_shift).astype(BF16)
    pre_act = jnp.einsum("td,gdf->tgf", normed_two, w_up, preferred_element_type=F32) + up_all.reshape(nt, -1)
    activated_full, gelu_back = jax.vjp(lambda a: jax.nn.gelu(a, approximate=False), pre_act)
    activated = activated_full.astype(BF16)
    mlp_out = jnp.einsum("tgf,gfd->td", activated, w_down, preferred_element_type=F32)
    result = (hidden + mlp_out + down_bias).astype(BF16)

    cot32 = cot.astype(F32)
    down_grad = jnp.einsum("tgf,td->gfd", activated, cot, preferred_element_type=F32).astype(BF16)
    grad_act = jnp.einsum("td,gfd->tgf", cot, w_down, preferred_element_type=F32)
    grad_pre = gelu_back(grad_act)[0].astype(BF16)
    up_bias_grad = jnp.sum(grad_pre.astype(F32), axis=0)
    up_grad = jnp.einsum("td,tgf->gdf", normed_two, grad_pre, preferred_element_type=F32).astype(BF16)
    grad_two = jnp.einsum("tgf,gdf->td", grad_pre, w_up, preferred_element_type=F32)
    second_gain_grad = jnp.sum(grad_two * xhat2, axis=0)
    second_shift_grad = jnp.sum(grad_two, axis=0)
    grad_hidden = cot32 + norm_back(grad_two * second_gain, xhat2, r2)
    out_bias_grad = jnp.sum(grad_hidden, axis=0)
    grad_branch = grad_hidden.astype(BF16)
    out_grad = jnp.einsum("tgc,td->gcd", heads_groups, grad_branch, preferred_element_type=F32).astype(BF16)
    grad_heads = jnp.einsum("td,gcd->tgc", grad_branch, w_out, preferred_element_type=F32).astype(BF16)
    grad_heads = grad_heads.reshape(own, width)

    products = (grad_heads.astype(F32) * heads_out.astype(F32)).reshape(own // BLOCK, BLOCK, width // 128, 2, HEAD_DIM)
    delta = jnp.sum(products, axis=-1).transpose(2, 0, 3, 1).reshape(width // 128, own // BLOCK, 1, 2 * BLOCK)
    stats = jnp.concatenate([lse, delta], axis=2)
    upward = [(i, i + 1) for i in range(nt - 1)]
    downward = [(i + 1, i) for i in range(nt - 1)]
    span = HALO // BLOCK
    g_all = jnp.concatenate([
        lax.ppermute(grad_heads[own - HALO:], "tensor", upward), grad_heads,
        lax.ppermute(grad_heads[:HALO], "tensor", downward)], axis=0)
    stats_all = jnp.concatenate([
        lax.ppermute(stats[:, own // BLOCK - span:], "tensor", upward), stats,
        lax.ppermute(stats[:, :span], "tensor", downward)], axis=1)
    dq, dk, dv = attend_back(q, k, v, g_all, stats_all[:, :, :1], stats_all[:, :, 1:], segc, segr, own)

    grad_qkv = jnp.stack([dq, dk, dv])
    normed_own = normed[own_rows]
    split = grad_qkv.reshape(3, own, nt, local)
    qkv_grad = jnp.einsum("stgc,td->gscd", split, normed_own, preferred_element_type=F32).astype(BF16)
    grad_normed = jnp.einsum("stgc,gscd->td", split, w_qkv, preferred_element_type=F32)
    xhat1, r1 = xhat_all[own_rows], r_all[own_rows]
    first_gain_grad = jnp.sum(grad_normed * xhat1, axis=0)
    first_shift_grad = jnp.sum(grad_normed, axis=0)
    input_grad = (grad_hidden + norm_back(grad_normed * first_gain, xhat1, r1)).astype(BF16)

    small = jnp.concatenate([
        jnp.stack([first_gain_grad, first_shift_grad, out_bias_grad, second_gain_grad, second_shift_grad,
                   jnp.sum(cot32, axis=0), jnp.sum(dq.astype(F32), axis=0), jnp.sum(dv.astype(F32), axis=0)]),
        up_bias_grad.reshape(-1, width)], axis=0)
    small = jnp.pad(small, ((0, -small.shape[0] % 8), (0, 0)))
    grads = jnp.concatenate([qkv_grad.reshape(nt, 3 * local, width), out_grad, up_grad, down_grad], axis=1)
    grads = grads.reshape((nt,) + pack.shape)
    extra = []
    bit = 8
    while bit < ndp:
        extra.append(bit)
        bit *= 2
    total, small, outs = reduce_grads(grads, small, jnp.stack([result, input_grad]), nt, tuple(extra))
    total = total.reshape(chunks * width, width).astype(F32) / ndp
    small = small / ndp
    up_rows = hidden_local // width
    return (
        outs[0].reshape(length, width),
        outs[1].reshape(length, width),
        small[0],
        small[1],
        total[:3 * local].reshape(3, local, width).transpose(0, 2, 1),
        lax.dynamic_slice_in_dim(small[6:8], t * local, local, axis=1),
        total[3 * local:width],
        small[2],
        small[3],
        small[4],
        total[width:2 * width],
        lax.dynamic_slice_in_dim(small, 8 + t * up_rows, up_rows).reshape(-1),
        total[2 * width:],
        small[5],
    )


def solution(mesh):
    placed = (
        P("dp", None), P("dp", None), P(), P(), P(None, None, "tensor"), P(None, "tensor"), P("tensor", None), P(),
        P(), P(), P(None, "tensor"), P("tensor"), P("tensor", None), P(), P("dp", None),
    )
    return jax.shard_map(
        body,
        mesh=mesh,
        in_specs=placed,
        out_specs=(
            P("dp", None), P("dp", None), P(), P(), P(None, None, "tensor"), P(None, "tensor"), P("tensor", None),
            P(), P(), P(), P(None, "tensor"), P("tensor"), P("tensor", None), P(),
        ),
        check_vma=False,
    )
```

time: 784 us -> 402 us (0.51)
  waiting for transfers between devices: 439 us -> 0.01 us
  Pallas kernels: 0 us -> 222 us
  matrix products: 130 us -> 53.2 us
  other arithmetic: 115 us -> 45.5 us
  between operations: 14.5 us -> 1.84 us
    psum x4 -> x0, waiting for transfers between devices: 439 us -> none  [the longest x1 168 us: body(): lax.psum(jnp.dot(activated, down_weight, preferred_element_type=jnp.float...]
    pallas_call x0 -> x4, Pallas kernels: none -> 222 us  [the longest x1 126 us: reduce_grads(): pl.pallas_call(functools.partial(reduce_kernel, nt, chunks, extra, outs),...]
    dot_general x32 -> x13, matrix products: 129 us -> 50.1 us  [the longest x3 7.05 us: project(): jnp.einsum('td,gcd->tgc', normed, w_qkv[:, s], preferred_element_type=F32)]
    reduce_sum x13 -> x6, other arithmetic: 37.3 us -> 5.21 us  [the longest x1 1.68 us: standardize(): center = rows - jnp.mean(rows, axis=-1, keepdims=True)]
    convert_element_type x7 -> x3, other arithmetic: 44.3 us -> 13.9 us  [the longest x1 11.6 us: body(): activated = activated_full.astype(BF16)]
    all_gather x0 -> x2, blocking collectives: none -> 27 us  [the longest x1 13.8 us: body(): qv_bias = lax.all_gather(query_value_bias, 'tensor', axis=1, tiled=True)]
    psum x1 -> x0, blocking collectives: 25.3 us -> none  [body(): lax.psum((first_gain_grad, first_shift_grad, qkv_weight_grad, query_value...]
    slice x3 -> x14, local copies, waits for them, and re-layouts: 3.21 us -> 16.1 us  [the longest x1 2.5 us: body(): outs[1].reshape(length, width)]
  transfers between devices with their start and end apart: 4 -> 4, of which waited for: 4 -> 0; matrix products, arithmetic and copies ran while one was open for 4% -> 6% of each run, Pallas kernels for 0% -> 0%
where the time goes in v1:
time: 402 us; the launch traced here: 395 us
  Pallas kernels  222 us (55%)
  matrix products  53.2 us (13%)
  other arithmetic  45.5 us (11%)
  local copies, waits for them, and re-layouts  36.4 us (9%)
  blocking collectives  27 us (7%)
  starting transfers between devices  9.54 us (2%)
    pallas_call x1, Pallas kernels, reduce_grads(): pl.pallas_call(functools.partial(reduce_kernel, nt, chunks, extra, outs),...  126 us
    pallas_call x1, Pallas kernels, gather_weights(): pl.pallas_call(functools.partial(gather_kernel, nt, chunks), name='gather...  62 us
    pallas_call x1, Pallas kernels, attend(): pl.pallas_call(functools.partial(attend_kernel, own), name='attend', out_...  17.3 us
    pallas_call x1, Pallas kernels, attend_back(): pl.pallas_call(functools.partial(attend_back_kernel, own), name='attend_b...  16.5 us
    all_gather x1, blocking collectives, body(): qv_bias = lax.all_gather(query_value_bias, 'tensor', axis=1, tiled=True)  13.8 us
    all_gather x1, blocking collectives, body(): up_all = lax.all_gather(up_bias, 'tensor', tiled=True)  13.2 us
    convert_element_type x1, other arithmetic, body(): activated = activated_full.astype(BF16)  11.6 us
  transfers between devices with their start and end apart: 4, of which 0 were waited for; matrix products, arithmetic and copies ran while one was open for 6% of the time, Pallas kernels for 0%

profile of v1, /device:TPU:0, one launch (start us, length us, event | category | flops | bytes accessed | tf_op | source)
XLA Modules:
  0.0 395.2 jit_solution(7986940216616152717)
XLA Ops:
  0.7 1.7 convert_reduce_fusion.1
  2.6 2.0 fusion.62
  7.7 13.8 %all-gather = f32[4,192,2]{1,2,0:T(2,128)S(1)} all-gather(f32[1,192,2]{1,2,0:T(2,128)} %bitcast.157), channel_id=1, replica_groups=mesh['dp'=8,'tensor'=4] {'tensor'}, dimensions={0}, use_global_device_ids=true | all-gather | bytes 7680 | tf_op jit(solution)/shard_map/all_gather | solution.py:572
  23.0 13.2 %all-gather.1 = f32[4,1,768]{2,1,0:T(1,128)S(1)} all-gather(f32[1,1,768]{2,1,0:T(1,128)} %reshape.165), channel_id=1, replica_groups=mesh['dp'=8,'tensor'=4] {'tensor'}, dimensions={0}, use_global_device_ids=true | all-gather | bytes 15360 | tf_op jit(solution)/shard_map/all_gather | solution.py:571
  36.2 3.3 pad_maximum_fusion.1
  39.5 62.0 %gather_weights.1 = bf16[4,3,2,2,2,2,48,768]{7,6,5,4,3,2,1,0:T(8,128)(2,1)} custom-call(bf16[3,2,2,2,2,48,768]{6,5,4,3,2,1,0:T(8,128)(2,1)} %bitcast.122), custom_call_target="tpu_custom_call" | custom-call | tf_op jit(solution)/shard_map/gather_weights/pallas_call | solution.py:174
  101.5 2.2 slice.145
  104.0 1.5 copy-done.1
  105.5 2.2 subtract_multiply_fusion
  107.7 2.3 convolution_convert_fusion.1.k_ref
  110.1 2.3 add_convert_fusion.1.v_ref
  112.4 2.4 add_convert_fusion.2.q_ref
  115.8 17.3 %attend.1 = (bf16[384,768]{1,0:T(8,128)(2,1)}, f32[6,3,1,256]{3,2,1,0:T(1,128)}) custom-call(bf16[896,768]{1,0:T(8,128)(2,1)} %add_convert_fusion.2.q_ref, bf16[896,768]{1,0:T(8,128)(2,1)} %convolution_convert_fusion.1.k_ref, bf16[896,768]{1,0:T(8,128)(2,1)} %add_convert_fusion.1.v_ref, s32[896,128]{1,0:T(8,128)} %broadcast_in_dim.4.segc, ...), custom_call_target="tpu_custom_call" | custom-call | tf_op jit(solution)/shard_map/attend/pallas_call | solution.py:482
  133.1 1.4 copy.55
  134.5 2.6 fusion.70
  137.4 5.4 %fusion.42 = (u8[384,768]{1,0:T(8,128)(4,1)S(1)}, u8[384,768]{1,0:T(8,128)(4,1)S(1)}, f32[384,4,768]{2,0,1:T(8,128)S(1)}) fusion(f32[4,768]{1,0:T(4,128)S(1)} %bitcast.153, bf16[4,2304,768]{2,1,0:T(8,128)(2,1)} %bitcast.112, f32[384,768]{1,0:T(8,128)S(1)} %get-tuple-element.70, f32[768]{0:T(1024)S(1)} %copy-done.37, f32[768]{0:T(1024)S(1)} %copy-done.31, ...), kind=kOutput, calls=%fused_computation.74 | convolution fusion | flops 1829339136 | bytes 11228160 | tf_op jit(solution)/shard_map/td,gdf->tgf/dot_general | solution.py:599
  142.9 11.6 %multiply_convert_fusion = (bf16[384,4,768]{2,0,1:T(8,128)(2,1)}, f32[384,4,768]{2,0,1:T(8,128)S(1)}) fusion(f32[384,4,768]{2,0,1:T(8,128)S(1)} %get-tuple-element.71, f32[4,768]{1,0:T(4,128)S(1)} %bitcast.154, u8[384,768]{1,0:T(8,128)(4,1)S(1)} %get-tuple-element.31, u8[384,768]{1,0:T(8,128)(4,1)S(1)} %get-tuple-element.30), kind=kLoop, calls=%fused_computation.10 | loop fusion | flops 83755008 | bytes 12398592 | tf_op jit(solution)/shard_map/convert_element_type | solution.py:601
  154.5 6.3 %convert_reduce_fusion = (f32[4,768]{1,0:T(4,128)}, bf16[384,4,768]{2,0,1:T(8,128)(2,1)}) fusion(f32[384,4,768]{2,0,1:T(8,128)S(1)} %get-tuple-element.52, bf16[4,2304,768]{2,1,0:T(8,128)(2,1)S(1)} %bitcast.116, bf16[1536,768]{1,0:T(8,128)(2,1)} %param.29, s32[]{:T(128)S(6)} %select_n.14, f32[384,4,768]{2,0,1:T(8,128)S(1)} %get-tuple-element.71, ...), kind=kOutput, calls=%fused_computation.9 | convolution fusion | flops 1831990272 | bytes 17129476 | tf_op jit(solution)/shard_map/td,gfd->tgf/dot_general | solution.py:607
  160.8 5.0 %multiply_reduce_fusion.2 = (f32[768]{0:T(1024)}, f32[384]{0:T(512)S(1)}, f32[384]{0:T(512)S(1)}, f32[768]{0:T(1024)}, f32[384,768]{1,0:T(8,128)S(1)}) fusion(f32[384,768]{1,0:T(8,128)} %copy-done.6, f32[384]{0:T(512)S(1)} %add_rsqrt_fusion.1, f32[384]{0:T(512)S(1)} %broadcast_multiply_fusion.6, f32[768]{0:T(1024)S(1)} %copy-done.31, ...), kind=kOutput, calls=%fused_computation.67 | convolution fusion | flops 1814591232 | bytes 9454592 | tf_op jit(solution)/shard_map/tgf,gdf->td/dot_general | solution.py:611
  165.8 1.6 fusion.63
  168.5 1.4 convert_multiply_fusion.1
  169.9 1.4 copy.60
  171.3 2.1 reshape.157
  173.8 1.4 collective-permute-start.2
  175.2 1.5 collective-permute-start.3
  177.5 1.9 copy.57
  179.4 1.3 collective-permute-start.1
  181.7 5.3 %collective-permute-start = (bf16[256,768]{1,0:T(8,128)(2,1)}, bf16[256,768]{1,0:T(8,128)(2,1)S(1)}, u32[]{:S(2)}, u32[]{:S(2)}) collective-permute-start(bf16[256,768]{1,0:T(8,128)(2,1)} %copy.56), channel_id=1, source_target_pairs={{0,1},{1,2},{2,3},{4,5},{5,6},{6,7},{8,9},{9,10},{10,11},{12,13},{... | collective-permute-start | bytes 1179656 | tf_op jit(solution)/shard_map/ppermute | solution.py:628
  187.0 6.2 %convert_bitcast_fusion = bf16[4,768,768]{2,1,0:T(8,128)(2,1)} fusion(bf16[384,4,768]{2,0,1:T(8,128)(2,1)} %get-tuple-element.75, f32[384,768]{1,0:T(8,128)S(1)} %copy-done.8, f32[768]{0:T(1024)S(1)} %copy-done.38, f32[768]{0:T(1024)S(1)} %copy-done.32, f32[384]{0:T(512)S(1)} %copy-done.29, f32[384]{0:T(512)S(1)} %broadcast_multiply_fusion.6), kind=kOutput, calls=%fused_computation.11 | convolution fusion | flops 1815773184 | bytes 8266752 | tf_op jit(solution)/shard_map/td,tgf->gdf/dot_general | solution.py:610
  193.2 5.3 %convolution_convert_fusion = bf16[4,768,768]{2,1,0:T(8,128)(2,1)} fusion(bf16[384,4,768]{2,0,1:T(8,128)(2,1)S(1)} %copy-done.10, bf16[1536,768]{1,0:T(8,128)(2,1)} %param.29, s32[]{:T(128)S(6)} %select_n.14), kind=kOutput, calls=%fused_computation.36 | convolution fusion | flops 1814298624 | bytes 7667716 | tf_op jit(solution)/shard_map/tgf,td->gfd/dot_general | solution.py:606
  198.6 5.2 %fusion.38 = bf16[1,384,768]{2,1,0:T(8,128)(2,1)} fusion(f32[384,768]{1,0:T(8,128)S(1)} %copy-done.8, bf16[384,4,768]{2,0,1:T(8,128)(2,1)S(1)} %copy-done.10, bf16[4,2304,768]{2,1,0:T(8,128)(2,1)} %bitcast.113, f32[768]{0:T(1024)S(1)} %copy-done.39), kind=kOutput, calls=%fused_computation.61 | convolution fusion | flops 1812824064 | bytes 8850432 | tf_op jit(solution)/shard_map/tgf,gfd->td/dot_general | solution.py:602
  203.8 1.8 convolution_convert_fusion.2
  208.2 2.2 pad_maximum_fusion.3.g_ref
  210.3 16.5 %attend_back.1 = (bf16[384,768]{1,0:T(8,128)(2,1)}, bf16[384,768]{1,0:T(8,128)(2,1)}, bf16[384,768]{1,0:T(8,128)(2,1)}) custom-call(bf16[896,768]{1,0:T(8,128)(2,1)} %add_convert_fusion.2.q_ref, bf16[896,768]{1,0:T(8,128)(2,1)} %convolution_convert_fusion.1.k_ref, bf16[896,768]{1,0:T(8,128)(2,1)} %add_convert_fusion.1.v_ref, ...), custom_call_target="tpu_custom_call" | custom-call | tf_op jit(solution)/shard_map/attend_back/pallas_call | solution.py:537
  226.8 1.3 convert_reduce_fusion.4
  228.1 1.4 copy.62
  229.5 1.2 convert_reduce_fusion.3
  234.0 1.5 pad_maximum_fusion.2
  235.5 4.4 %multiply_reduce_fusion.1 = (f32[384]{0:T(512)S(1)}, f32[768]{0:T(1024)S(1)}, f32[384]{0:T(512)S(1)}, f32[768]{0:T(1024)S(1)}, f32[384,768]{1,0:T(8,128)}) fusion(f32[896,768]{1,0:T(8,128)} %get-tuple-element.60, f32[768]{0:T(1024)S(1)} %copy-done.25, bf16[4,3,192,768]{3,2,1,0:T(8,128)(2,1)S(1)} %bitcast.120, bf16[1,384,4,192]{1,3,2,0:T(8,128)(2,1)} %bitcast.134, ...), kind=kOutput, calls=%fused_computation.64 | convolution fusion | flops 1362786048 | bytes 7680000 | tf_op jit(solution)/shard_map/stgc,gscd->td/dot_general | solution.py:639
  239.9 1.5 concatenate.24
  242.0 3.1 fusion.47
  247.0 2.4 fusion.46
  250.5 6.5 %pad_maximum_fusion = bf16[4,2304,768]{2,1,0:T(8,128)(2,1)} fusion(bf16[4,768,768]{2,1,0:T(8,128)(2,1)S(1)} %bitcast.128, bf16[4,768,768]{2,1,0:T(8,128)(2,1)S(1)} %bitcast.126, bf16[4,192,768]{2,1,0:T(8,128)(2,1)S(1)} %copy-done.5, bf16[4,576,768]{2,1,0:T(8,128)(2,1)S(1)} %bitcast.121), kind=kLoop, calls=%fused_computation | loop fusion | flops 56623104 | bytes 28311552 | tf_op jit(solution)/shard_map/concatenate | solution.py:650
  257.1 126.0 %reduce_grads.1 = (bf16[3,2,2,2,2,48,768]{6,5,4,3,2,1,0:T(8,128)(2,1)}, f32[16,768]{1,0:T(8,128)}, bf16[2,4,384,768]{3,2,1,0:T(8,128)(2,1)}) custom-call(bf16[4,3,2,2,2,2,48,768]{7,6,5,4,3,2,1,0:T(8,128)(2,1)} %bitcast.106, f32[16,768]{1,0:T(8,128)} %pad.14.small, bf16[2,384,768]{2,1,0:T(8,128)(2,1)} %pad_maximum_fusion.4.own_rows), custom_call_target="tpu_custom_call" | custom-call | tf_op jit(solution)/shard_map/reduce_grads/pallas_call | solution.py:402
  383.0 2.9 convert_multiply_fusion
  386.8 1.3 slice.165
  388.1 2.5 fusion.65
  390.9 2.5 fusion.66
  (155 shorter events, 21.5 us)
Async XLA Ops:
  0.6 2.0 copy-start
  2.6 2.0 copy-start.33
  2.6 33.6 %copy-start.14 = (bf16[768,768]{1,0:T(8,128)(2,1)S(1)}, bf16[768,768]{1,0:T(8,128)(2,1)}, u32[]{:S(2)}) copy-start(bf16[768,768]{1,0:T(8,128)(2,1)} %param.27) | copy-start | bytes 3538948
  7.2 15.8 %copy-start.20 = (s32[896]{0:T(1024)}, s32[896]{0:T(1024)S(1)}, u32[]{:S(2)}) copy-start(s32[896]{0:T(1024)S(1)} %pad_dynamic-slice_fusion.1) | copy-start | bytes 10756
  103.7 1.8 copy-start.1
  107.7 4.7 %copy-start.9 = (bf16[896,768]{1,0:T(8,128)(2,1)}, bf16[896,768]{1,0:T(8,128)(2,1)S(1)}, u32[]{:S(2)}) copy-start(bf16[896,768]{1,0:T(8,128)(2,1)S(1)} %get-tuple-element.61) | copy-start | bytes 4128772
  112.4 2.4 copy-start.21
  115.7 18.7 %copy-start.36 = (f32[768]{0:T(1024)S(1)}, f32[768]{0:T(1024)}, u32[]{:S(2)}) copy-start(f32[768]{0:T(1024)} %param.22) | copy-start | bytes 9220
  134.4 2.9 copy-start.12
  134.5 2.9 copy-start.31
  134.5 2.9 copy-start.37
  137.1 5.8 %copy-start.6 = (f32[384,768]{1,0:T(8,128)}, f32[384,768]{1,0:T(8,128)S(1)}, u32[]{:S(2)}) copy-start(f32[384,768]{1,0:T(8,128)S(1)} %get-tuple-element.70) | copy-start | bytes 3538948
  137.4 28.4 %copy-start.28 = (f32[384]{0:T(512)}, f32[384]{0:T(512)S(1)}, u32[]{:S(2)}) copy-start(f32[384]{0:T(512)S(1)} %add_rsqrt_fusion.1) | copy-start | bytes 4612
  137.4 17.1 %slice-start = ((s8[14155776]{0:T(1024)(128)(4,1)}), s8[4194304]{0:T(1024)(128)(4,1)S(1)}, s32[]{:S(2)}) async-start(s8[14155776]{0:T(1024)(128)(4,1)} %bitcast.114), calls=%async_computation | async-start | bytes 8388608
  137.4 17.1 %slice-start.1 = ((s8[14155776]{0:T(1024)(128)(4,1)}), s8[4194304]{0:T(1024)(128)(4,1)S(1)}, s32[]{:S(2)}) async-start(s8[14155776]{0:T(1024)(128)(4,1)} %bitcast.114), calls=%async_computation.1 | async-start | bytes 8388608
  137.4 17.0 %slice-start.2 = ((s8[14155776]{0:T(1024)(128)(4,1)}), s8[4194304]{0:T(1024)(128)(4,1)S(1)}, s32[]{:S(2)}) async-start(s8[14155776]{0:T(1024)(128)(4,1)} %bitcast.114), calls=%async_computation.2 | async-start | bytes 8388608
  142.9 11.6 %slice-start.3 = ((s8[14155776]{0:T(1024)(128)(4,1)}), s8[1572864]{0:T(1024)(128)(4,1)S(1)}, s32[]{:S(2)}) async-start(s8[14155776]{0:T(1024)(128)(4,1)} %bitcast.114), calls=%async_computation.3 | async-start | bytes 3145728
  160.8 5.0 %copy-start.7 = (f32[384,768]{1,0:T(8,128)S(1)}, f32[384,768]{1,0:T(8,128)}, u32[]{:S(2)}) copy-start(f32[384,768]{1,0:T(8,128)} %copy-done.6) | copy-start | bytes 3538948
  171.3 2.4 copy-start.18
  173.4 13.6 %copy-start.29 = (f32[384]{0:T(512)S(1)}, f32[384]{0:T(512)}, u32[]{:S(2)}) copy-start(f32[384]{0:T(512)} %copy-done.28) | copy-start | bytes 4612
  173.4 13.6 %copy-start.32 = (f32[768]{0:T(1024)S(1)}, f32[768]{0:T(1024)}, u32[]{:S(2)}) copy-start(f32[768]{0:T(1024)} %param.23) | copy-start | bytes 9220
  173.4 13.6 %copy-start.38 = (f32[768]{0:T(1024)S(1)}, f32[768]{0:T(1024)}, u32[]{:S(2)}) copy-start(f32[768]{0:T(1024)} %param.24) | copy-start | bytes 9220
  173.7 13.4 %copy-start.8 = (f32[384,768]{1,0:T(8,128)S(1)}, f32[384,768]{1,0:T(8,128)}, u32[]{:S(2)}) copy-start(f32[384,768]{1,0:T(8,128)} %copy-done.6) | copy-start | bytes 3538948
  173.8 33.6 %collective-permute-start.2 = (f32[6,2,2,256]{3,2,1,0:T(2,128)S(1)}, f32[6,2,2,256]{3,2,1,0:T(2,128)S(1)}, u32[]{:S(2)}, u32[]{:S(2)}) collective-permute-start(f32[6,2,2,256]{3,2,1,0:T(2,128)S(1)} %get-tuple-element.67), channel_id=1, source_target_pairs={{0,1},{1,2},{2,3},{4,5},{5,6},{6,7},{8,9},{9,10},{10,11},{12,13},{... | collective-permute-start | bytes 73736 | tf_op jit(solution)/shard_map/ppermute | solution.py:631
  175.2 32.2 %collective-permute-start.3 = (f32[6,2,2,256]{3,2,1,0:T(2,128)S(1)}, f32[6,2,2,256]{3,2,1,0:T(2,128)S(1)}, u32[]{:S(2)}, u32[]{:S(2)}) collective-permute-start(f32[6,2,2,256]{3,2,1,0:T(2,128)S(1)} %get-tuple-element.68), channel_id=1, source_target_pairs={{1,0},{2,1},{3,2},{5,4},{6,5},{7,6},{9,8},{10,9},{11,10},{13,12},{... | collective-permute-start | bytes 73736 | tf_op jit(solution)/shard_map/ppermute | solution.py:632
  179.4 28.7 %collective-permute-start.1 = (bf16[256,768]{1,0:T(8,128)(2,1)}, bf16[256,768]{1,0:T(8,128)(2,1)}, u32[]{:S(2)}, u32[]{:S(2)}) collective-permute-start(bf16[256,768]{1,0:T(8,128)(2,1)} %copy.57), channel_id=1, source_target_pairs={{1,0},{2,1},{3,2},{5,4},{6,5},{7,6},{9,8},{10,9},{11,10},{13,12},{... | collective-permute-start | bytes 1179656 | tf_op jit(solution)/shard_map/ppermute | solution.py:629
  181.7 11.6 %copy-start.10 = (bf16[384,4,768]{2,0,1:T(8,128)(2,1)S(1)}, bf16[384,4,768]{2,0,1:T(8,128)(2,1)}, u32[]{:S(2)}) copy-start(bf16[384,4,768]{2,0,1:T(8,128)(2,1)} %get-tuple-element.51) | copy-start | bytes 7077892
  181.7 26.5 %collective-permute-start = (bf16[256,768]{1,0:T(8,128)(2,1)}, bf16[256,768]{1,0:T(8,128)(2,1)S(1)}, u32[]{:S(2)}, u32[]{:S(2)}) collective-permute-start(bf16[256,768]{1,0:T(8,128)(2,1)} %copy.56), channel_id=1, source_target_pairs={{0,1},{1,2},{2,3},{4,5},{5,6},{6,7},{8,9},{9,10},{10,11},{12,13},{... | collective-permute-start | bytes 1179656 | tf_op jit(solution)/shard_map/ppermute | solution.py:628
  193.2 5.3 %copy-start.39 = (f32[768]{0:T(1024)S(1)}, f32[768]{0:T(1024)}, u32[]{:S(2)}) copy-start(f32[768]{0:T(1024)} %param.28) | copy-start | bytes 9220
  198.6 5.2 %copy-start.13 = (bf16[384,768]{0,1:T(8,128)(2,1)S(1)}, bf16[384,768]{0,1:T(8,128)(2,1)}, u32[]{:S(2)}) copy-start(bf16[384,768]{0,1:T(8,128)(2,1)} %copy-done.12) | copy-start | bytes 1769476
  203.8 1.8 copy-start.23
  203.8 2.4 copy-start.35
  203.8 2.4 copy-start.34
  203.8 4.4 %copy-start.4 = (bf16[384,768]{1,0:T(8,128)(2,1)S(1)}, bf16[384,768]{1,0:T(8,128)(2,1)}, u32[]{:S(2)}) copy-start(bf16[384,768]{1,0:T(8,128)(2,1)} %copy-done.3) | copy-start | bytes 1769476
  226.8 3.8 copy-start.11
  226.8 4.9 %copy-start.16 = (bf16[384,768]{1,0:T(8,128)(2,1)S(1)}, bf16[384,768]{1,0:T(8,128)(2,1)}, u32[]{:S(2)}) copy-start(bf16[384,768]{1,0:T(8,128)(2,1)} %get-tuple-element.25) | copy-start | bytes 1769476
  230.7 4.8 %copy-start.25 = (f32[768]{0:T(1024)S(1)}, f32[768]{0:T(1024)}, u32[]{:S(2)}) copy-start(f32[768]{0:T(1024)} %param.17) | copy-start | bytes 9220
  232.8 2.7 copy-start.2
  235.5 4.4 %copy-start.26 = (f32[1,768]{1,0:T(1,128)S(1)}, f32[1,768]{1,0:T(1,128)}, u32[]{:S(2)}) copy-start(f32[1,768]{1,0:T(1,128)} %stack.51) | copy-start | bytes 9220
  245.1 5.4 %slice-start.4 = ((s8[4718592]{0:T(1024)(128)(4,1)}), s8[4194304]{0:T(1024)(128)(4,1)S(1)}, s32[]{:S(2)}) async-start(s8[4718592]{0:T(1024)(128)(4,1)} %bitcast.125), calls=%async_computation.4 | async-start | bytes 8388608
  245.1 5.4 %slice-start.6 = ((s8[4718592]{0:T(1024)(128)(4,1)}), s8[4194304]{0:T(1024)(128)(4,1)S(1)}, s32[]{:S(2)}) async-start(s8[4718592]{0:T(1024)(128)(4,1)} %bitcast.127), calls=%async_computation.6 | async-start | bytes 8388608
  245.5 5.0 %slice-start.5 = ((s8[4718592]{0:T(1024)(128)(4,1)}), s8[524288]{0:T(1024)(128)(4,1)S(1)}, s32[]{:S(2)}) async-start(s8[4718592]{0:T(1024)(128)(4,1)} %bitcast.125), calls=%async_computation.5 | async-start | bytes 1048576
  245.5 5.0 %slice-start.7 = ((s8[4718592]{0:T(1024)(128)(4,1)}), s8[524288]{0:T(1024)(128)(4,1)S(1)}, s32[]{:S(2)}) async-start(s8[4718592]{0:T(1024)(128)(4,1)} %bitcast.127), calls=%async_computation.7 | async-start | bytes 1048576
  245.8 3.6 copy-start.17
  247.0 3.5 copy-start.5
  386.8 3.8 slice-start.8
  388.1 2.8 slice-start.9
  390.9 2.5 copy-start.19
  (6 other events, 9.8 us)

commit v2 on v1

--- a/solution.py
+++ b/solution.py
@@ -57,7 +57,7 @@
         task()
 
 
-def relay_tasks(nt, chunks, own, full, sems, start, hop, place_of, arrived):
+def relay_tasks(nt, chunks, own, full, sems, start, arrived):
     send, recv = sems
     tasks = []
     t = lax.axis_index("tensor")
@@ -97,95 +97,6 @@
     return tasks, finish
 
 
-def gather_kernel(nt, chunks, pack, w, zs, zr, ps, pr, cs, cr, ls):
-    d, t, b0, b1, b2 = place()
-    local = pltpu.make_async_copy(pack, w.at[t], ls)
-    local.start()
-    greet(nt, (1, 2, 4))
-    tasks = []
-
-    def one(shard, k, q, way, j):
-        if q == 0:
-            return remote(w.at[shard, k, b0, b2, b1, 0], w.at[shard, k, b0, b2, b1, 0],
-                       ps.at[k, j, way, 0], pr.at[k, j, way, 0], dp=flip(d, 2))
-        return remote(w.at[shard, k, b0, b2, b1, 1], w.at[shard, k, b0, b2, b1, 1],
-                   ps.at[k, j, way, 1], pr.at[k, j, way, 1], dp=flip(d, 4))
-
-    def two(shard, k, q, way, j):
-        if q == 0:
-            return remote(w.at[shard, k, b0, b2, :, 0], w.at[shard, k, b0, b2, :, 0],
-                       ps.at[k, j, way, 2], pr.at[k, j, way, 2], dp=flip(d, 4))
-        return remote(w.at[shard, k, b0, :, b1, 1], w.at[shard, k, b0, :, b1, 1],
-                   ps.at[k, j, way, 3], pr.at[k, j, way, 3], dp=flip(d, 2))
-
-    def core(shard, k, way, j):
-        return remote(w.at[shard, k, b0], w.at[shard, k, b0], cs.at[k, j, way], cr.at[k, j, way], dp=flip(d, 1))
-
-    def arrived(k, j, way, shard):
-        one(shard, k, 0, way, j - 1).start()
-        one(shard, k, 1, way, j - 1).start()
-
-    def each(k, j, body):
-        for way in (0, 1):
-            shard = t - (1 - 2 * way) * (j + 1)
-            @pl.when((shard >= 0) & (shard < nt))
-            def _():
-                body(shard, k, way, j)
-
-    z_tasks, z_finish = relay_tasks(
-        nt, chunks, lambda k: pack.at[k, b0, b2, b1], lambda s, k: w.at[s, k, b0, b2, b1], (zs, zr),
-        lambda k, j: 16.0 * k + 4.0 * j, None, None, arrived)
-    tasks += z_tasks
-    for k in range(chunks):
-        for j in range(nt - 1):
-            def second(k=k, j=j):
-                def body(shard, k, way, j):
-                    for q in (0, 1):
-                        one(shard, k, q, way, j).wait_recv()
-                    for q in (0, 1):
-                        two(shard, k, q, way, j).start()
-                each(k, j, body)
-
-            def third(k=k, j=j):
-                def body(shard, k, way, j):
-                    for q in (0, 1):
-                        two(shard, k, q, way, j).wait_recv()
-                    core(shard, k, way, j).start()
-                each(k, j, body)
-            tasks.append((16.0 * k + 4.0 * j + 9.0, len(tasks), second))
-            tasks.append((16.0 * k + 4.0 * j + 16.5, len(tasks), third))
-    ordered(tasks)
-    local.wait()
-    z_finish()
-    for k in range(chunks):
-        for j in range(nt - 1):
-            def last(shard, k, way, j):
-                core(shard, k, way, j).wait()
-                for q in (0, 1):
-                    one(shard, k, q, way, j).wait_send()
-                    two(shard, k, q, way, j).wait_send()
-            each(k, j, last)
-
-
-def gather_weights(pack, nt):
-    chunks, rows = pack.shape[0], pack.shape[-2]
-    width = pack.shape[-1]
-    dma = pltpu.SemaphoreType.DMA
-    return pl.pallas_call(
-        functools.partial(gather_kernel, nt, chunks),
-        name="gather_weights",
-        out_shape=jax.ShapeDtypeStruct((nt,) + pack.shape, pack.dtype),
-        in_specs=[pl.BlockSpec(memory_space=pl.ANY)],
-        out_specs=pl.BlockSpec(memory_space=pltpu.VMEM),
-        scratch_shapes=[
-            dma((chunks, nt - 1, 2)), dma((chunks, nt - 1, 2)),
-            dma((chunks, nt - 1, 2, 4)), dma((chunks, nt - 1, 2, 4)),
-            dma((chunks, nt - 1, 2)), dma((chunks, nt - 1, 2)), dma(()),
-        ],
-        compiler_params=pltpu.CompilerParams(collective_id=1, has_side_effects=True, vmem_limit_bytes=VMEM_LIMIT),
-    )(pack)
-
-
 def add_bf16(ref, other):
     ref[...] = (ref[...].astype(F32) + other[...].astype(F32)).astype(BF16)
 
@@ -349,7 +260,7 @@
 
     z_tasks, z_finish = relay_tasks(
         nt, outs, lambda o: own_rows.at[o], lambda s, o: gathered.at[o, s], (os_, or_),
-        lambda o, j: 1.0 + 46.0 * o + 14.0 * j, None, None, lambda *a: None)
+        lambda o, j: 1.0 + 46.0 * o + 14.0 * j, lambda *a: None)
     tasks += [(w, 1000 + n, b) for w, n, b in z_tasks]
 
     exchanges = [("dp", bit) for bit in bits]
@@ -450,44 +361,6 @@
     return jnp.concatenate([both[:HEAD_DIM, :half], both[HEAD_DIM:, half:]], axis=0).T
 
 
-def attend_kernel(own, q_ref, k_ref, v_ref, segc, segr, o_ref, lse_ref):
-    blocks = own // BLOCK
-    for b in range(blocks):
-        first, count = BLOCK * b, BLOCK + 2 * HALO
-        q0 = HALO + BLOCK * b
-        row = segr[:, q0:q0 + BLOCK]
-        allowed = segc[first:first + count, :] == row
-        allowed = jnp.concatenate([allowed, allowed], axis=1)
-
-        def pair(j, carry):
-            cols = pl.ds(pl.multiple_of(j * 128, 128), 128)
-            q2 = stacked(q_ref[q0:q0 + BLOCK, cols])
-            k2 = k_ref[first:first + count, cols]
-            v2 = v_ref[first:first + count, cols]
-            s = dot(k2, q2, NT) * (HEAD_DIM ** -0.5)
-            s = jnp.where(allowed, s, -1e9)
-            m = jnp.max(s, axis=0, keepdims=True)
-            p = jnp.exp(s - m)
-            l = jnp.sum(p, axis=0, keepdims=True)
-            low = (p * (1.0 / l)).astype(BF16)
-            out = dot(v2.T, low, NN)
-            o_ref[b * BLOCK:(b + 1) * BLOCK, cols] = untangle(out).astype(BF16)
-            lse_ref[j, b] = m + jnp.log(l)
-            return carry
-        lax.fori_loop(0, q_ref.shape[1] // 128, pair, 0)
-
-
-def attend(q, k, v, segc, segr, own):
-    width = q.shape[1]
-    return pl.pallas_call(
-        functools.partial(attend_kernel, own),
-        name="attend",
-        out_shape=(jax.ShapeDtypeStruct((own, width), BF16),
-                   jax.ShapeDtypeStruct((width // 128, own // BLOCK, 1, 2 * BLOCK), F32)),
-        compiler_params=pltpu.CompilerParams(vmem_limit_bytes=VMEM_LIMIT),
-    )(q, k, v, segc, segr)
-
-
 def attend_back_kernel(own, q_ref, k_ref, v_ref, g_ref, lse_ref, delta_ref, segc, segr, dq_ref, dk_ref, dv_ref, dk, dv):
     scale = HEAD_DIM ** -0.5
     window = own + 2 * HALO
@@ -553,6 +426,384 @@
     return r * (e - jnp.mean(e, axis=-1, keepdims=True) - xhat * jnp.mean(e * xhat, axis=-1, keepdims=True))
 
 
+def grid_rows(block):
+    return block.reshape(-1, block.shape[-1])
+
+
+def nearest(nt):
+    return [sorted(range(nt), key=lambda s: (abs(s - p), s if p < nt // 2 else -s)) for p in range(nt)]
+
+
+def pick(table, position):
+    t = lax.axis_index("tensor")
+    return sum((t == p).astype(jnp.int32) * row[position] for p, row in enumerate(table))
+
+
+def gelu_parts(x):
+    cdf = 0.5 * (1.0 + lax.erf(x * (0.5 ** 0.5)))
+    pdf = jnp.exp(-0.5 * x * x) * ((2.0 * jnp.pi) ** -0.5)
+    return x * cdf, cdf + x * pdf
+
+
+Z_TIMES = ((0.0, 4.0, 8.0, 12.0), (16.0, 24.0, 32.0, 40.0), (20.0, 28.0, 36.0, 44.0))
+
+
+def forward_kernel(nt, chunks, own,
+                   tok, cot, segc, segr, vecs, bias, pack,
+                   result, grad_hidden, q_ref, k_ref, v_ref, normed, g_ref, stats, small, out_g, grads, w0,
+                   w, bias_all, bias_sem, bias_recv, heads, heads_t, hidden, normed_two, n2t, cot_t, mlp, gtwo,
+                   gbuf, pre_s, gact_s, act, gpre, gsem, zs, zr, ps, pr, cs, cr, ls):
+    d, t, b0, b1, b2 = place()
+    window, width = tok.shape
+    local = width // nt
+    blocks = own // BLOCK
+    local_copy = pltpu.make_async_copy(pack, w.at[t], ls.at[0])
+    local_copy.start()
+    bias_copy = pltpu.make_async_copy(bias, bias_all.at[t], ls.at[1])
+    bias_copy.start()
+
+    barrier = pltpu.get_barrier_semaphore()
+    for bit in (1, 2, 4):
+        pl.semaphore_signal(barrier, inc=1, device_id={"dp": flip(d, bit)}, device_id_type=MESH)
+    for j in range(1, nt):
+        pl.semaphore_signal(barrier, inc=1, device_id={"tensor": lax.rem(t + j, nt)}, device_id_type=MESH)
+    pl.semaphore_wait(barrier, 3 + nt - 1)
+    tasks = []
+
+    def task(when, body):
+        tasks.append((when, len(tasks), body))
+
+    def bias_send(j):
+        return remote(bias, bias_all.at[t], bias_sem.at[j], bias_recv.at[j], tensor=lax.rem(t + j + 1, nt))
+
+    def bias_get(j):
+        source = lax.rem(t + nt - j - 1, nt)
+        return remote(bias, bias_all.at[source], bias_sem.at[j], bias_recv.at[j], tensor=source)
+
+    def one(shard, k, q, way, j):
+        if q == 0:
+            return remote(w.at[shard, k, b0, b2, b1, 0], w.at[shard, k, b0, b2, b1, 0],
+                          ps.at[k, j, way, 0], pr.at[k, j, way, 0], dp=flip(d, 2))
+        return remote(w.at[shard, k, b0, b2, b1, 1], w.at[shard, k, b0, b2, b1, 1],
+                      ps.at[k, j, way, 1], pr.at[k, j, way, 1], dp=flip(d, 4))
+
+    def two(shard, k, q, way, j):
+        if q == 0:
+            return remote(w.at[shard, k, b0, b2, :, 0], w.at[shard, k, b0, b2, :, 0],
+                          ps.at[k, j, way, 2], pr.at[k, j, way, 2], dp=flip(d, 4))
+        return remote(w.at[shard, k, b0, :, b1, 1], w.at[shard, k, b0, :, b1, 1],
+                      ps.at[k, j, way, 3], pr.at[k, j, way, 3], dp=flip(d, 2))
+
+    def core(shard, k, way, j):
+        return remote(w.at[shard, k, b0], w.at[shard, k, b0], cs.at[k, j, way], cr.at[k, j, way], dp=flip(d, 1))
+
+    def arrived(k, j, way, shard):
+        one(shard, k, 0, way, j - 1).start()
+        one(shard, k, 1, way, j - 1).start()
+
+    def each(k, j, act):
+        for way in (0, 1):
+            shard = t - (1 - 2 * way) * (j + 1)
+
+            @pl.when((shard >= 0) & (shard < nt))
+            def _():
+                act(shard, k, way, j)
+
+    z_tasks, z_finish = relay_tasks(
+        nt, chunks, lambda k: pack.at[k, b0, b2, b1], lambda s, k: w.at[s, k, b0, b2, b1], (zs, zr),
+        lambda k, j: Z_TIMES[k][j], arrived)
+    tasks += z_tasks
+    for k in range(chunks):
+        for j in range(nt - 1):
+            def second(k=k, j=j):
+                def act(shard, k, way, j):
+                    for q in (0, 1):
+                        one(shard, k, q, way, j).wait_recv()
+                    for q in (0, 1):
+                        two(shard, k, q, way, j).start()
+                each(k, j, act)
+
+            def third(k=k, j=j):
+                def act(shard, k, way, j):
+                    for q in (0, 1):
+                        two(shard, k, q, way, j).wait_recv()
+                    core(shard, k, way, j).start()
+                each(k, j, act)
+
+            def fourth(k=k, j=j):
+                def act(shard, k, way, j):
+                    core(shard, k, way, j).wait_recv()
+                each(k, j, act)
+            arrive = Z_TIMES[k][j + 1]
+            task(arrive + 5.0, second)
+            task(arrive + 12.0, third)
+            task(arrive + 16.0, fourth)
+
+    def bias_begin():
+        for j in range(nt - 1):
+            bias_send(j).start()
+
+    def bias_end():
+        bias_copy.wait()
+        for j in range(nt - 1):
+            bias_get(j).wait_recv()
+    task(0.2, bias_begin)
+    task(10.0, bias_end)
+
+    g1, s1, ob, g2, s2, db = (vecs[i:i + 1, :] for i in range(6))
+
+    for i in range(window // BLOCK):
+        def norm_rows(i=i):
+            def part(n, carry):
+                rows = pl.ds(pl.multiple_of(i * BLOCK + n * 32, 32), 32)
+                xhat, _ = standardize(tok[rows, :].astype(F32))
+                normed[rows, :] = (xhat * g1 + s1).astype(BF16)
+                return carry
+            lax.fori_loop(0, BLOCK // 32, part, 0)
+        task(0.5 + 0.7 * i, norm_rows)
+
+    def transposes():
+        cot_t[...] = cot[...].T
+        small[5:6, :] = jnp.sum(cot[...].astype(F32), axis=0, keepdims=True)
+    task(6.0, transposes)
+
+    half_rows = window // 2
+    group = 2 * local
+
+    def project(u, kind, part):
+        rows = slice(part * half_rows, (part + 1) * half_rows)
+        weight = w[pl.ds(2 * u, 2), 0, kind // 2, kind % 2].reshape(group, width)
+        out = dot(normed[rows, :], weight, NT)
+        if kind != 1:
+            line = 1 + kind // 2
+            out = out + jnp.concatenate([bias_all[2 * u, line:line + 1, :local], bias_all[2 * u + 1, line:line + 1, :local]], axis=1)
+        target = (q_ref, k_ref, v_ref)[kind]
+        target[rows, pl.ds(pl.multiple_of(u * group, 128), group)] = out.astype(BF16)
+
+    def attention(u, b):
+        first, count = BLOCK * b + 32, BLOCK + 448
+        q0 = HALO + BLOCK * b
+        allowed = segc[first:first + count, :] == segr[:, q0:q0 + BLOCK]
+        allowed = jnp.concatenate([allowed, allowed], axis=1)
+
+        def pair(j, carry):
+            at = u * (group // 128) + j
+            cols = pl.ds(pl.multiple_of(at * 128, 128), 128)
+            q2 = stacked(q_ref[q0:q0 + BLOCK, cols])
+            k2 = k_ref[first:first + count, cols]
+            v2 = v_ref[first:first + count, cols]
+            s = dot(k2, q2, NT) * (HEAD_DIM ** -0.5)
+            s = jnp.where(allowed, s, -1e9)
+            m = jnp.max(s, axis=0, keepdims=True)
+            p = jnp.exp(s - m)
+            l = jnp.sum(p, axis=0, keepdims=True)
+            low = (p * (1.0 / l)).astype(BF16)
+            out = dot(v2.T, low, NN)
+            half = out.shape[1] // 2
+            both = jnp.concatenate([out[:HEAD_DIM, :half], out[HEAD_DIM:, half:]], axis=0).astype(BF16)
+            heads_t[cols, b * BLOCK:(b + 1) * BLOCK] = both
+            heads[b * BLOCK:(b + 1) * BLOCK, cols] = both.T
+            stats[at, b, 0:1, :] = m + jnp.log(l)
+            return carry
+        lax.fori_loop(0, group // 128, pair, 0)
+
+    def out_project(u, fresh):
+        weight = w[pl.ds(2 * u, 2), 0, 1, 1].reshape(group, width)
+        part = dot(heads[:, pl.ds(pl.multiple_of(u * group, 128), group)], weight, NN)
+        if fresh:
+            hidden[...] = part
+        else:
+            hidden[...] += part
+
+    first_half = t // 2
+    at = 7.0
+    for n in range(nt // 2):
+        u = lax.rem(first_half + n, nt // 2)
+        if n == 0:
+            def own_ready():
+                local_copy.wait()
+            task(20.8, own_ready)
+            at = 20.9
+        else:
+            at = max(at, 28.5)
+        for kind in range(3):
+            for part in range(2):
+                def run(u=u, kind=kind, part=part):
+                    project(u, kind, part)
+                task(at, run)
+                at += 0.7
+        for b in range(blocks):
+            def run(u=u, b=b):
+                attention(u, b)
+            task(at, run)
+            at += 3.0
+
+        def run(u=u, n=n):
+            out_project(u, n == 0)
+        task(at, run)
+        at += 0.6
+
+    def rows_of(i):
+        return slice(i * BLOCK, (i + 1) * BLOCK)
+
+    for i in range(blocks):
+        def norm_two(i=i):
+            rows = rows_of(i)
+            token = tok[HALO + i * BLOCK:HALO + (i + 1) * BLOCK, :].astype(F32)
+            whole = hidden[rows, :] + token + ob
+            hidden[rows, :] = whole
+            xhat, _ = standardize(whole)
+            low = (xhat * g2 + s2).astype(BF16)
+            normed_two[rows, :] = low
+            n2t[:, rows] = low.T
+        task(at, norm_two)
+        at += 0.7
+
+    table = nearest(nt)
+    slab = 32
+
+    def grads_out(slot, shard):
+        return pltpu.make_async_copy(gbuf.at[slot], grads.at[shard], gsem.at[slot])
+
+    def mlp_shard(position, shard):
+        slot = position % 2
+        up = w[shard, 1].reshape(width, width)
+        down = w[shard, 2].reshape(width, width)
+        pre_s[...] = dot(normed_two[...], up, NN) + bias_all[shard, 0:1, :]
+        gact_s[...] = dot(cot[...], down, NT)
+
+        def step(i, total):
+            rows = pl.ds(pl.multiple_of(i * slab, slab), slab)
+            value, slope = gelu_parts(pre_s[rows, :])
+            act[rows, :] = value.astype(BF16)
+            low = (gact_s[rows, :] * slope).astype(BF16)
+            gpre[rows, :] = low
+            return total + low.astype(F32)
+        total = lax.fori_loop(0, own // slab, step, jnp.zeros((slab, width), F32))
+        small[pl.ds(8 + shard, 1), :] = jnp.sum(total, axis=0, keepdims=True)
+        if position == 0:
+            mlp[...] = dot(act[...], down, NN)
+            gtwo[...] = dot(gpre[...], up, NT)
+        else:
+            mlp[...] += dot(act[...], down, NN)
+            gtwo[...] += dot(gpre[...], up, NT)
+        if position >= 2:
+            grads_out(slot, shard).wait()
+        gbuf[slot, 0] = dot(n2t[...], gpre[...], NN).astype(BF16).reshape(gbuf.shape[2:])
+        gbuf[slot, 1] = dot(cot_t[...], act[...], NN).astype(BF16).reshape(gbuf.shape[2:])
+        grads_out(slot, shard).start()
+
+    for position in range(nt):
+        def run(position=position):
+            mlp_shard(position, pick(table, position))
+        if position > 0:
+            at = max(at, Z_TIMES[2][position] + 16.5)
+        task(at, run)
+        at += 6.0
+
+    for i in range(blocks):
+        def finish_rows(i=i):
+            rows = rows_of(i)
+            whole = hidden[rows, :]
+            result[rows, :] = (whole + mlp[rows, :] + db).astype(BF16)
+            xhat, r = standardize(whole)
+            grad = gtwo[rows, :]
+            gh = cot[rows, :].astype(F32) + norm_back(grad * g2, xhat, r)
+            grad_hidden[rows, :] = gh
+            sums = (jnp.sum(gh, axis=0, keepdims=True), jnp.sum(grad * xhat, axis=0, keepdims=True),
+                    jnp.sum(grad, axis=0, keepdims=True))
+            for n, value in enumerate(sums):
+                if i == 0:
+                    small[2 + n:3 + n, :] = value
+                else:
+                    small[2 + n:3 + n, :] += value
+            normed_two[rows, :] = gh.astype(BF16)
+        task(at, finish_rows)
+        at += 0.8
+
+    def out_back():
+        outw = w[:, 0, 1, 1].reshape(width, width)
+        branch = normed_two[...]
+        g_ref[...] = dot(branch, outw, NT).astype(BF16)
+        g_t = dot(outw, branch, NT).astype(BF16).astype(F32)
+        product = g_t * heads_t[...].astype(F32)
+        for h in range(width // HEAD_DIM):
+            line = jnp.sum(product[h * HEAD_DIM:(h + 1) * HEAD_DIM, :], axis=0, keepdims=True)
+            for b in range(blocks):
+                stats[h // 2, b, 1:2, (h % 2) * BLOCK:(h % 2 + 1) * BLOCK] = line[:, b * BLOCK:(b + 1) * BLOCK]
+    task(at, out_back)
+
+    def out_grad():
+        out_g[...] = dot(heads_t[...], normed_two[...], NN).astype(BF16)
+    task(at + 2.0, out_grad)
+
+    def keep_copy():
+        return pltpu.make_async_copy(w.at[:, 0], w0, ls.at[0])
+
+    def keep_first():
+        keep_copy().start()
+    task(at - 0.1, keep_first)
+    ordered(tasks)
+    grads_out(0, 0).wait()
+    grads_out(1, 0).wait()
+    keep_copy().wait()
+    for n in (0, 1, 6, 7):
+        small[n:n + 1, :] = jnp.zeros((1, width), F32)
+    if small.shape[0] > 8 + nt:
+        small[8 + nt:, :] = jnp.zeros((small.shape[0] - 8 - nt, width), F32)
+    z_finish()
+    for j in range(nt - 1):
+        bias_send(j).wait_send()
+    for k in range(chunks):
+        for j in range(nt - 1):
+            def end(shard, k, way, j):
+                core(shard, k, way, j).wait_send()
+                for q in (0, 1):
+                    one(shard, k, q, way, j).wait_send()
+                    two(shard, k, q, way, j).wait_send()
+            each(k, j, end)
+
+
+def forward(tok, cot, segc, segr, vecs, bias, pack, nt):
+    chunks, piece, width = pack.shape[0], pack.shape[-2], pack.shape[-1]
+    window, own = tok.shape[0], cot.shape[0]
+    lines = 8 + nt + -nt % 8
+    dma = pltpu.SemaphoreType.DMA
+    vmem, any_ = pl.BlockSpec(memory_space=pltpu.VMEM), pl.BlockSpec(memory_space=pl.ANY)
+
+    def shape(dims, kind):
+        return jax.ShapeDtypeStruct(dims, kind)
+    return pl.pallas_call(
+        functools.partial(forward_kernel, nt, chunks, own),
+        name="forward",
+        out_shape=(
+            shape((own, width), BF16), shape((own, width), F32),
+            shape((window, width), BF16), shape((window, width), BF16), shape((window, width), BF16),
+            shape((window, width), BF16), shape((own, width), BF16),
+            shape((width // 128, own // BLOCK, 2, 2 * BLOCK), F32), shape((lines, width), F32),
+            shape((width, width), BF16), shape((nt, chunks - 1) + pack.shape[1:], BF16),
+            shape((nt,) + pack.shape[1:], BF16),
+        ),
+        in_specs=[vmem] * 6 + [any_],
+        out_specs=(vmem,) * 10 + (any_, any_),
+        scratch_shapes=[
+            pltpu.VMEM((nt,) + pack.shape, BF16), pltpu.VMEM((nt,) + bias.shape, F32), dma((nt - 1,)), dma((nt - 1,)),
+            pltpu.VMEM((own, width), BF16), pltpu.VMEM((width, own), BF16), pltpu.VMEM((own, width), F32),
+            pltpu.VMEM((own, width), BF16), pltpu.VMEM((width, own), BF16), pltpu.VMEM((width, own), BF16),
+            pltpu.VMEM((own, width), F32), pltpu.VMEM((own, width), F32),
+            pltpu.VMEM((2, chunks - 1) + pack.shape[1:], BF16),
+            pltpu.VMEM((own, width), F32), pltpu.VMEM((own, width), F32),
+            pltpu.VMEM((own, width), BF16), pltpu.VMEM((own, width), BF16),
+            dma((2,)),
+            dma((chunks, nt - 1, 2)), dma((chunks, nt - 1, 2)),
+            dma((chunks, nt - 1, 2, 4)), dma((chunks, nt - 1, 2, 4)),
+            dma((chunks, nt - 1, 2)), dma((chunks, nt - 1, 2)), dma((2,)),
+        ],
+        compiler_params=pltpu.CompilerParams(
+            collective_id=1, has_side_effects=True, vmem_limit_bytes=VMEM_LIMIT),
+    )(tok, cot, segc, segr, vecs, bias, pack)
+
+
 def body(tokens_in, segment_ids, first_gain, first_shift, qkv_weight, query_value_bias, out_weight, out_bias,
          second_gain, second_shift, up_weight, up_bias, down_weight, down_bias, cotangent):
     nt, ndp = lax.axis_size("tensor"), lax.axis_size("dp")
@@ -567,60 +818,18 @@
     piece = width // 16
     pack = pack.reshape(-1, 2, 2, 2, 2, piece, width)
     chunks = pack.shape[0]
-    whole = gather_weights(pack, nt).reshape(nt, chunks * width, width)
-    up_all = lax.all_gather(up_bias, "tensor", tiled=True)
-    qv_bias = lax.all_gather(query_value_bias, "tensor", axis=1, tiled=True)
-    w_qkv = whole[:, :3 * local].reshape(nt, 3, local, width)
-    w_out = whole[:, 3 * local:width]
-    w_up = whole[:, width:2 * width]
-    w_down = whole[:, 2 * width:]
-
     padded = jnp.pad(tokens_in, ((HALO, HALO), (0, 0)))
-    tokens = lax.dynamic_slice_in_dim(padded, start, own + 2 * HALO).astype(F32)
+    tokens = lax.dynamic_slice_in_dim(padded, start, own + 2 * HALO)
     segs = lax.dynamic_slice_in_dim(jnp.pad(segment_ids[0], (HALO, HALO), constant_values=-1), start, own + 2 * HALO)
     segr = segs[None, :]
     segc = jnp.broadcast_to(segs[:, None], (own + 2 * HALO, BLOCK))
     cot = lax.dynamic_slice_in_dim(cotangent, start, own)
-    xhat_all, r_all = standardize(tokens)
-    normed = (xhat_all * first_gain + first_shift).astype(BF16)
+    vecs = jnp.pad(jnp.stack([first_gain, first_shift, out_bias, second_gain, second_shift, down_bias]), ((0, 2), (0, 0)))
+    bias = jnp.pad(jnp.concatenate([up_bias[None], jnp.pad(query_value_bias, ((0, 0), (0, width - local)))]), ((0, 5), (0, 0)))
+    result, grad_hidden, q, k, v, normed, grad_heads, stats, small1, out_grad, mlp_grads, w_first = forward(
+        tokens, cot, segc, segr, vecs, bias, pack, nt)
     own_rows = slice(HALO, HALO + own)
-
-    def project(s):
-        return jnp.einsum("td,gcd->tgc", normed, w_qkv[:, s], preferred_element_type=F32).reshape(-1, width)
-    q = (project(0) + qv_bias[0]).astype(BF16)
-    k = project(1).astype(BF16)
-    v = (project(2) + qv_bias[1]).astype(BF16)
-    heads_out, lse = attend(q, k, v, segc, segr, own)
-    heads_groups = heads_out.reshape(own, nt, local)
-    branch = jnp.einsum("tgc,gcd->td", heads_groups, w_out, preferred_element_type=F32)
-    hidden = tokens[own_rows] + branch + out_bias
-    xhat2, r2 = standardize(hidden)
-    normed_two = (xhat2 * second_gain + second_shift).astype(BF16)
-    pre_act = jnp.einsum("td,gdf->tgf", normed_two, w_up, preferred_element_type=F32) + up_all.reshape(nt, -1)
-    activated_full, gelu_back = jax.vjp(lambda a: jax.nn.gelu(a, approximate=False), pre_act)
-    activated = activated_full.astype(BF16)
-    mlp_out = jnp.einsum("tgf,gfd->td", activated, w_down, preferred_element_type=F32)
-    result = (hidden + mlp_out + down_bias).astype(BF16)
-
-    cot32 = cot.astype(F32)
-    down_grad = jnp.einsum("tgf,td->gfd", activated, cot, preferred_element_type=F32).astype(BF16)
-    grad_act = jnp.einsum("td,gfd->tgf", cot, w_down, preferred_element_type=F32)
-    grad_pre = gelu_back(grad_act)[0].astype(BF16)
-    up_bias_grad = jnp.sum(grad_pre.astype(F32), axis=0)
-    up_grad = jnp.einsum("td,tgf->gdf", normed_two, grad_pre, preferred_element_type=F32).astype(BF16)
-    grad_two = jnp.einsum("tgf,gdf->td", grad_pre, w_up, preferred_element_type=F32)
-    second_gain_grad = jnp.sum(grad_two * xhat2, axis=0)
-    second_shift_grad = jnp.sum(grad_two, axis=0)
-    grad_hidden = cot32 + norm_back(grad_two * second_gain, xhat2, r2)
-    out_bias_grad = jnp.sum(grad_hidden, axis=0)
-    grad_branch = grad_hidden.astype(BF16)
-    out_grad = jnp.einsum("tgc,td->gcd", heads_groups, grad_branch, preferred_element_type=F32).astype(BF16)
-    grad_heads = jnp.einsum("td,gcd->tgc", grad_branch, w_out, preferred_element_type=F32).astype(BF16)
-    grad_heads = grad_heads.reshape(own, width)
-
-    products = (grad_heads.astype(F32) * heads_out.astype(F32)).reshape(own // BLOCK, BLOCK, width // 128, 2, HEAD_DIM)
-    delta = jnp.sum(products, axis=-1).transpose(2, 0, 3, 1).reshape(width // 128, own // BLOCK, 1, 2 * BLOCK)
-    stats = jnp.concatenate([lse, delta], axis=2)
+    w_qkv = w_first.reshape(nt, width, width)[:, :3 * local].reshape(nt, 3, local, width)
     upward = [(i, i + 1) for i in range(nt - 1)]
     downward = [(i + 1, i) for i in range(nt - 1)]
     span = HALO // BLOCK
@@ -637,18 +846,15 @@
     split = grad_qkv.reshape(3, own, nt, local)
     qkv_grad = jnp.einsum("stgc,td->gscd", split, normed_own, preferred_element_type=F32).astype(BF16)
     grad_normed = jnp.einsum("stgc,gscd->td", split, w_qkv, preferred_element_type=F32)
-    xhat1, r1 = xhat_all[own_rows], r_all[own_rows]
+    xhat1, r1 = standardize(tokens[own_rows].astype(F32))
     first_gain_grad = jnp.sum(grad_normed * xhat1, axis=0)
     first_shift_grad = jnp.sum(grad_normed, axis=0)
     input_grad = (grad_hidden + norm_back(grad_normed * first_gain, xhat1, r1)).astype(BF16)
 
-    small = jnp.concatenate([
-        jnp.stack([first_gain_grad, first_shift_grad, out_bias_grad, second_gain_grad, second_shift_grad,
-                   jnp.sum(cot32, axis=0), jnp.sum(dq.astype(F32), axis=0), jnp.sum(dv.astype(F32), axis=0)]),
-        up_bias_grad.reshape(-1, width)], axis=0)
-    small = jnp.pad(small, ((0, -small.shape[0] % 8), (0, 0)))
-    grads = jnp.concatenate([qkv_grad.reshape(nt, 3 * local, width), out_grad, up_grad, down_grad], axis=1)
-    grads = grads.reshape((nt,) + pack.shape)
+    small = small1.at[:2].set(jnp.stack([first_gain_grad, first_shift_grad])).at[6:8].set(
+        jnp.stack([jnp.sum(dq.astype(F32), axis=0), jnp.sum(dv.astype(F32), axis=0)]))
+    first = jnp.concatenate([qkv_grad.reshape(nt, 3 * local, width), out_grad.reshape(nt, local, width)], axis=1)
+    grads = jnp.concatenate([first.reshape((nt, 1) + pack.shape[1:]), mlp_grads], axis=1)
     extra = []
     bit = 8
     while bit < ndp:
@@ -671,7 +877,7 @@
         small[4],
         total[width:2 * width],
         lax.dynamic_slice_in_dim(small, 8 + t * up_rows, up_rows).reshape(-1),
-        total[2 * width:],
+        total[2 * width:].T,
         small[5],
     )
 

time: 402 us -> 329 us (0.82)
  matrix products: 53.2 us -> 6.19 us
  blocking collectives: 27 us -> 0 us
  other arithmetic: 45.5 us -> 23.1 us
  Pallas kernels: 222 us -> 232 us
  local copies, waits for them, and re-layouts: 36.4 us -> 42.5 us
  waiting for transfers between devices: 0.01 us -> 5.7 us
  starting transfers between devices: 9.54 us -> 14.1 us
    dot_general x12 -> x0, matrix products: 45.7 us -> none  [the longest x3 7.05 us: project(): jnp.einsum('td,gcd->tgc', normed, w_qkv[:, s], preferred_element_type=F32)]
    all_gather x2 -> x0, blocking collectives: 27 us -> none  [the longest x1 13.8 us: body(): qv_bias = lax.all_gather(query_value_bias, 'tensor', axis=1, tiled=True)]
    convert_element_type x2 -> x0, other arithmetic: 13.5 us -> none  [the longest x1 11.6 us: body(): activated = activated_full.astype(BF16)]
    pallas_call x1, Pallas kernels: 16.5 us -> 24.9 us  [attend_back(): pl.pallas_call(functools.partial(attend_back_kernel, own), name='attend_b...]
    pallas_call x2 -> x1, Pallas kernels: 79.3 us -> 85.2 us  [forward(): pl.pallas_call(functools.partial(forward_kernel, nt, chunks, own), name='...]
    ppermute x1, starting transfers between devices: 1.42 us -> 6.27 us  [body(): lax.ppermute(stats[:, own // BLOCK - span:], 'tensor', upward)]
    another operation x8 -> x11, local copies, waits for them, and re-layouts: 2.34 us -> 7.05 us  [the longest x7 7.03 us: body(): jnp.stack([first_gain, first_shift, out_bias, second_gain, second_shift,...]
    ppermute x1, waiting for transfers between devices: 0.01 us -> 4.64 us  [body(): lax.ppermute(grad_heads[:HALO], 'tensor', downward)]
  transfers between devices with their start and end apart: 4 -> 4, of which waited for: 0 -> 2; matrix products, arithmetic and copies ran while one was open for 6% -> 2% of each run, Pallas kernels for 0% -> 0%
where the time goes in v2:
time: 329 us; the launch traced here: 325 us
  Pallas kernels  232 us (71%)
  local copies, waits for them, and re-layouts  42.5 us (13%)
  other arithmetic  23.1 us (7%)
  starting transfers between devices  14.1 us (4%)
  matrix products  6.19 us (2%)
  waiting for transfers between devices  5.7 us (2%)
    pallas_call x1, Pallas kernels, reduce_grads(): pl.pallas_call(functools.partial(reduce_kernel, nt, chunks, extra, outs),...  122 us
    pallas_call x1, Pallas kernels, forward(): pl.pallas_call(functools.partial(forward_kernel, nt, chunks, own), name='...  85.2 us
    pallas_call x1, Pallas kernels, attend_back(): pl.pallas_call(functools.partial(attend_back_kernel, own), name='attend_b...  24.9 us
    another operation x7, local copies, waits for them, and re-layouts, body(): jnp.stack([first_gain, first_shift, out_bias, second_gain, second_shift,...  7.03 us
  transfers between devices with their start and end apart: 4, of which 2 were waited for; matrix products, arithmetic and copies ran while one was open for 2% of the time, Pallas kernels for 0%

profile of v2, /device:TPU:0, one launch (start us, length us, event | category | flops | bytes accessed | tf_op | source)
XLA Modules:
  0.0 324.6 jit_solution(7336163096553305277)
XLA Ops:
  0.7 0.9 reduce.4
  2.2 2.6 pad_dynamic-slice_fusion.1.tok
  5.4 1.3 stack.62
  6.7 1.3 stack.63
  8.0 1.3 stack.64
  9.2 1.3 stack.65
  10.5 0.7 broadcast_in_dim.8
  11.2 1.4 stack.66
  12.6 1.4 pad.26.vecs
  14.0 0.7 select_maximum_fusion
  15.3 0.9 constant_dynamic-slice_fusion.1.cot
  16.2 3.1 pad_maximum_fusion.2
  19.3 1.0 broadcast_in_dim.6.segc
  20.2 85.2 %forward.1 = (bf16[384,768]{1,0:T(8,128)(2,1)}, f32[384,768]{1,0:T(8,128)}, bf16[896,768]{1,0:T(8,128)(2,1)}, bf16[896,768]{1,0:T(8,128)(2,1)}, bf16[896,768]{1,...) custom-call(bf16[896,768]{1,0:T(8,128)(2,1)} %pad_dynamic-slice_fusi, ...), custom_call_target="tpu_custom_call" | custom-call | tf_op jit(solution)/shard_map/forward/pallas_call | solution.py:776
  105.4 0.8 fusion.24
  106.2 6.3 %collective-permute-start.2 = (f32[6,2,2,256]{3,2,1,0:T(2,128)S(1)}, f32[6,2,2,256]{3,2,1,0:T(2,128)S(1)}, u32[]{:S(2)}, u32[]{:S(2)}) collective-permute-start(f32[6,2,2,256]{3,2,1,0:T(2,128)S(1)} %get-tuple-element.94), channel_id=1, source_target_pairs={{0,1},{1,2},{2,3},{4,5},{5,6},{6,7},{8,9},{9,10},{10,11},{12,13},{... | collective-permute-start | bytes 73736 | tf_op jit(solution)/shard_map/ppermute | solution.py:840
  112.5 1.3 collective-permute-start.3
  113.8 1.9 fusion.22
  115.7 5.3 %collective-permute-start = (bf16[256,768]{1,0:T(8,128)(2,1)}, bf16[256,768]{1,0:T(8,128)(2,1)}, u32[]{:S(2)}, u32[]{:S(2)}) collective-permute-start(bf16[256,768]{1,0:T(8,128)(2,1)} %get-tuple-element.89), channel_id=1, source_target_pairs={{0,1},{1,2},{2,3},{4,5},{5,6},{6,7},{8,9},{9,10},{10,11},{12,13},{... | collective-permute-start | bytes 1179656 | tf_op jit(solution)/shard_map/ppermute | solution.py:837
  121.0 1.3 collective-permute-start.1
  123.6 1.1 copy-done.5
  124.7 2.0 slice.132
  126.7 0.7 fusion.23
  127.4 1.1 collective-permute-done
  128.5 4.6 %collective-permute-done.1 = bf16[256,768]{1,0:T(8,128)(2,1)} collective-permute-done((bf16[256,768]{1,0:T(8,128)(2,1)S(1)}, bf16[256,768]{1,0:T(8,128)(2,1)}, u32[]{:S(2)}, u32[]{:S(2)}) %collective-permute-start.1) | collective-permute-done | bytes 393248 | tf_op jit(solution)/shard_map/ppermute | solution.py:838
  133.1 2.3 pad_maximum_fusion.4.g_ref
  135.4 24.9 %attend_back.1 = (bf16[384,768]{1,0:T(8,128)(2,1)}, bf16[384,768]{1,0:T(8,128)(2,1)}, bf16[384,768]{1,0:T(8,128)(2,1)}) custom-call(bf16[896,768]{1,0:T(8,128)(2,1)} %get-tuple-element.57.q_ref, bf16[896,768]{1,0:T(8,128)(2,1)} %get-tuple-element.58.k_ref, bf16[896,768]{1,0:T(8,128)(2,1)} %get-tuple-element.59.v_ref, ...), custom_call_target="tpu_custom_call" | custom-call | tf_op jit(solution)/shard_map/attend_back/pallas_call | solution.py:410
  160.3 1.4 copy.34
  161.7 1.4 copy.36
  163.1 1.4 convert_reduce_fusion.1
  164.5 2.1 copy.35
  166.6 1.4 pad_maximum_fusion.3
  168.1 0.7 copy-done.3
  168.8 3.1 fusion.11
  172.0 3.1 fusion.18
  175.7 1.0 copy-done.9
  177.2 0.9 copy-done.10
  178.1 1.1 pad_maximum_fusion.5.own_rows
  179.5 0.9 slice-done.1
  180.7 5.7 %pad_maximum_fusion.grads = bf16[4,3,2,2,2,2,48,768]{7,6,5,4,3,2,1,0:T(8,128)(2,1)} fusion(bf16[4,2,2,2,2,2,48,768]{7,6,5,4,3,2,1,0:T(8,128)(2,1)S(1)} %bitcast.43, bf16[4,1,2,2,2,2,48,768]{7,6,5,4,3,2,1,0:T(8,128)(2,1)S(1)} %bitcast.39), kind=kLoop, calls=%fused_computation | loop fusion | flops 7077888 | bytes 28311552 | tf_op jit(solution)/shard_map/concatenate | solution.py:857
  187.6 121.7 %reduce_grads.1 = (bf16[3,2,2,2,2,48,768]{6,5,4,3,2,1,0:T(8,128)(2,1)}, f32[16,768]{1,0:T(8,128)}, bf16[2,4,384,768]{3,2,1,0:T(8,128)(2,1)}) custom-call(bf16[4,3,2,2,2,2,48,768]{7,6,5,4,3,2,1,0:T(8,128)(2,1)} %pad_maximum_fusion.grads, f32[16,768]{1,0:T(8,128)} %maximum_dynamic-update-slice_fusion.1.small, bf16[2,384,768]{2,1,0:T(8,128)(2,1)} %pad_maximum_fusion.5.own_rows), custom_call_target="tpu_custom_call" | custom-call | tf_op jit(solution)/shard_map/reduce_grads/pallas_call | solution.py:313
  309.3 2.9 convert_multiply_fusion
  312.1 1.7 fusion.20
  313.9 1.3 slice.135
  315.2 0.9 slice.137
  316.0 1.9 copy.39
  318.0 5.0 %fusion.21 = (bf16[1,4,384,768]{3,2,1,0:T(8,128)(2,1)}, bf16[1,4,384,768]{3,2,1,0:T(8,128)(2,1)}) fusion(bf16[2,4,384,768]{3,2,1,0:T(8,128)(2,1)} %get-tuple-element.71), kind=kLoop, calls=%fused_computation.56 | loop fusion | bytes 9437184 | tf_op jit(solution)/shard_map/slice | solution.py:869
  323.0 0.7 slice_reduce_fusion
  (62 shorter events, 6.8 us)
Async XLA Ops:
  0.6 14.7 %copy-start = (bf16[1536,768]{1,0:T(8,128)(2,1)S(1)}, bf16[1536,768]{1,0:T(8,128)(2,1)}, u32[]{:S(2)}) copy-start(bf16[1536,768]{1,0:T(8,128)(2,1)} %param.33) | copy-start | bytes 7077892
  2.2 2.6 copy-start.13
  2.2 2.6 copy-start.15
  2.2 14.0 %copy-start.7 = (bf16[768,768]{1,0:T(8,128)(2,1)S(1)}, bf16[768,768]{1,0:T(8,128)(2,1)}, u32[]{:S(2)}) copy-start(bf16[768,768]{1,0:T(8,128)(2,1)} %param.31) | copy-start | bytes 3538948
  12.6 3.6 %copy-start.8 = (bf16[768,768]{1,0:T(8,128)(2,1)S(1)}, bf16[768,768]{1,0:T(8,128)(2,1)}, u32[]{:S(2)}) copy-start(bf16[768,768]{1,0:T(8,128)(2,1)} %param.29) | copy-start | bytes 3538948
  20.2 102.1 %copy-start.2 = (bf16[1536,768]{1,0:T(8,128)(2,1)S(1)}, bf16[1536,768]{1,0:T(8,128)(2,1)}, u32[]{:S(2)}) copy-start(bf16[1536,768]{1,0:T(8,128)(2,1)} %param.19) | copy-start | bytes 7077892
  106.2 20.4 %collective-permute-start.2 = (f32[6,2,2,256]{3,2,1,0:T(2,128)S(1)}, f32[6,2,2,256]{3,2,1,0:T(2,128)S(1)}, u32[]{:S(2)}, u32[]{:S(2)}) collective-permute-start(f32[6,2,2,256]{3,2,1,0:T(2,128)S(1)} %get-tuple-element.94), channel_id=1, source_target_pairs={{0,1},{1,2},{2,3},{4,5},{5,6},{6,7},{8,9},{9,10},{10,11},{12,13},{... | collective-permute-start | bytes 73736 | tf_op jit(solution)/shard_map/ppermute | solution.py:840
  112.5 14.2 %collective-permute-start.3 = (f32[6,2,2,256]{3,2,1,0:T(2,128)S(1)}, f32[6,2,2,256]{3,2,1,0:T(2,128)S(1)}, u32[]{:S(2)}, u32[]{:S(2)}) collective-permute-start(f32[6,2,2,256]{3,2,1,0:T(2,128)S(1)} %get-tuple-element.93), channel_id=1, source_target_pairs={{1,0},{2,1},{3,2},{5,4},{6,5},{7,6},{9,8},{10,9},{11,10},{13,12},{... | collective-permute-start | bytes 73736 | tf_op jit(solution)/shard_map/ppermute | solution.py:841
  115.7 12.8 %collective-permute-start = (bf16[256,768]{1,0:T(8,128)(2,1)}, bf16[256,768]{1,0:T(8,128)(2,1)}, u32[]{:S(2)}, u32[]{:S(2)}) collective-permute-start(bf16[256,768]{1,0:T(8,128)(2,1)} %get-tuple-element.89), channel_id=1, source_target_pairs={{0,1},{1,2},{2,3},{4,5},{5,6},{6,7},{8,9},{9,10},{10,11},{12,13},{... | collective-permute-start | bytes 1179656 | tf_op jit(solution)/shard_map/ppermute | solution.py:837
  121.0 12.1 %collective-permute-start.1 = (bf16[256,768]{1,0:T(8,128)(2,1)S(1)}, bf16[256,768]{1,0:T(8,128)(2,1)}, u32[]{:S(2)}, u32[]{:S(2)}) collective-permute-start(bf16[256,768]{1,0:T(8,128)(2,1)S(1)} %get-tuple-element.90), channel_id=1, source_target_pairs={{1,0},{2,1},{3,2},{5,4},{6,5},{7,6},{9,8},{10,9},{11,10},{13,12},{... | collective-permute-start | bytes 1179656 | tf_op jit(solution)/shard_map/ppermute | solution.py:838
  122.3 2.3 copy-start.5
  124.7 2.0 copy-start.11
  124.7 8.5 %copy-start.4 = (bf16[384,768]{1,0:T(8,128)(2,1)S(1)}, bf16[384,768]{1,0:T(8,128)(2,1)}, u32[]{:S(2)}) copy-start(bf16[384,768]{1,0:T(8,128)(2,1)} %get-tuple-element.60) | copy-start | bytes 1769476
  166.6 2.2 copy-start.3
  175.4 1.3 copy-start.9
  175.4 1.3 copy-start.14
  175.5 4.1 %slice-start = ((s8[9437184]{0:T(1024)(128)(4,1)}), s8[4194304]{0:T(1024)(128)(4,1)S(1)}, s32[]{:S(2)}) async-start(s8[9437184]{0:T(1024)(128)(4,1)} %bitcast.42), calls=%async_computation | async-start | bytes 8388608
  176.7 1.4 copy-start.10
  176.7 3.7 %slice-start.1 = ((s8[9437184]{0:T(1024)(128)(4,1)}), s8[4194304]{0:T(1024)(128)(4,1)S(1)}, s32[]{:S(2)}) async-start(s8[9437184]{0:T(1024)(128)(4,1)} %bitcast.42), calls=%async_computation.1 | async-start | bytes 8388608
  177.2 2.0 copy-start.6
  179.2 1.5 slice-start.2
  318.0 5.0 %copy-start.12 = (f32[16,768]{1,0:T(8,128)S(1)}, f32[16,768]{1,0:T(8,128)}, u32[]{:S(2)}) copy-start(f32[16,768]{1,0:T(8,128)} %get-tuple-element.72) | copy-start | bytes 147460
  318.0 6.3 %copy-start.1 = (bf16[1536,768]{1,0:T(8,128)(2,1)S(1)}, bf16[1536,768]{1,0:T(8,128)(2,1)}, u32[]{:S(2)}) copy-start(bf16[1536,768]{1,0:T(8,128)(2,1)} %param.33) | copy-start | bytes 7077892
